TPU v7x, 128 devices: a whole 4x4x4 slice. The times are simulated.
128 devices in a mesh: ctx: 8 (over x_lo, y), exp: 16 (over z, x_hi, core).
Axes of the slice: x: 4 (x_hi: 2, x_lo: 2; x = x_hi * 2 + x_lo), y: 4, z: 4, core: 2. Of those that a mesh axis runs over, the one named last changes fastest.
Arguments:
- queries: bfloat16 [16, 1024, 4096], P('exp', 'ctx'), may hold values from -6 to 6
- keys: bfloat16 [16, 1024, 512], P('exp', 'ctx'), may hold values from -6 to 6
- values: bfloat16 [16, 1024, 512], P('exp', 'ctx'), may hold values from -8 to 8
- resid: bfloat16 [16, 1024, 2048], P('exp', 'ctx'), may hold values from -40 to 40
- out_weight: bfloat16 [4096, 2048], P('ctx', 'exp'), may hold values from -0.5 to 0.5
- norm_gain: float32 [2048], replicated, may hold values from 0.5 to 2
- expert_gate: bfloat16 [32, 2048, 768], P('exp'), may hold values from -0.125 to 0.125
- expert_up: bfloat16 [32, 2048, 768], P('exp'), may hold values from -0.125 to 0.125
- expert_down: bfloat16 [32, 768, 2048], P('exp'), may hold values from -0.4375 to 0.4375
- route_ids: int32 [16, 1024, 8], P('exp', 'ctx'), may hold values from 0 to 31, as said below
- route_gates: float32 [16, 1024, 8], P('exp', 'ctx'), may hold values from 0.1 to 1
Outputs:
- attn_resid: bfloat16 [16, 1024, 2048], P('exp', 'ctx')
- layer_out: bfloat16 [16, 1024, 2048], P('exp', 'ctx')
Inputs may be any that keep to these rules, and one draw needn't show every extreme that they name: `route_ids`: each row names 8 different experts. In every block of 128 consecutive positions of a sequence (the tokens of one device) each expert is named by at most 64 rows, and one expert, the same in all blocks of a draw, by exactly 64 rows.
All inputs are finite; a program needn't handle non-finite values.
Results may differ from a plain program's by a relative error of at most 0.017.
Values may be sent and summed in bfloat16 or wider, within the bound.
A program may use at most 128 MiB of HBM per device.

v0:
```python
import jax
import jax.numpy as jnp
from jax import lax
from jax.sharding import PartitionSpec as P

QUERY_HEAD_COUNT = 32
KEY_VALUE_HEADS = 4
HEAD_SIZE = 128
TOPK = 8
CAP = 64


norm_eps = 1e-06
mask_fill_value = -1e30


def from_behind(shard, axis, by):
    devices = lax.axis_size(axis)
    pairs = [(i, i + by) for i in range(devices) if 0 <= i + by < devices]
    return lax.ppermute(shard, axis, pairs)


def attend_block(state_now, key_value_portion, begin_row, query_head_rows, query_place):
    row_top, row_total, accum = state_now
    key_total = key_value_portion.shape[1]
    key_head_rows = key_value_portion[0].reshape(key_total, KEY_VALUE_HEADS, HEAD_SIZE)
    value_head_rows = key_value_portion[1].reshape(key_total, KEY_VALUE_HEADS, HEAD_SIZE)
    raw_scores = jnp.einsum(
        "tngd,und->ngtu", query_head_rows, key_head_rows, preferred_element_type=jnp.float32
    ) * HEAD_SIZE ** (-0.5)
    key_place = begin_row + jnp.arange(key_total, dtype=jnp.int32)
    allowed = query_place[:, None] >= key_place[None, :]
    raw_scores = jnp.where(allowed, raw_scores, mask_fill_value)
    new_top = jnp.maximum(row_top, jnp.max(raw_scores, axis=-1))
    factor = jnp.exp(row_top - new_top)
    exp_scores = jnp.where(allowed, jnp.exp(raw_scores - new_top[..., None]), 0.0)
    row_total = row_total * factor + jnp.sum(exp_scores, axis=-1)
    weights = exp_scores.astype(jnp.bfloat16)
    accum = accum * factor[..., None] + jnp.einsum(
        "ngtu,und->ngtd", weights, value_head_rows, preferred_element_type=jnp.float32
    )
    return (new_top, row_total, accum)


def experts_apply(arrived, gate_local, up_local, down_local):
    gate_part = jnp.einsum(
        "secd,edf->secf", arrived, gate_local, preferred_element_type=jnp.float32
    )
    up_part = jnp.einsum("secd,edf->secf", arrived, up_local, preferred_element_type=jnp.float32)
    activated = (jax.nn.silu(gate_part) * up_part).astype(jnp.bfloat16)
    return jnp.einsum(
        "secf,efd->secd", activated, down_local, preferred_element_type=jnp.float32
    ).astype(jnp.bfloat16)


def local(
    queries,
    keys,
    values,
    resid,
    out_weight,
    norm_gain,
    expert_gate,
    expert_up,
    expert_down,
    route_ids,
    route_gates,
):
    token_rows = queries.shape[1]
    ctx_count = lax.axis_size("ctx")
    exp_count = lax.axis_size("exp")
    my_block = lax.axis_index("ctx")
    query_group = QUERY_HEAD_COUNT // KEY_VALUE_HEADS
    query_head_rows = queries[0].reshape(token_rows, KEY_VALUE_HEADS, query_group, HEAD_SIZE)
    query_place = my_block * token_rows + jnp.arange(token_rows, dtype=jnp.int32)
    kv_local = jnp.stack([keys[0], values[0]])
    state_first = (
        jnp.full((KEY_VALUE_HEADS, query_group, token_rows), mask_fill_value, jnp.float32),
        jnp.zeros((KEY_VALUE_HEADS, query_group, token_rows), jnp.float32),
        jnp.zeros((KEY_VALUE_HEADS, query_group, token_rows, HEAD_SIZE), jnp.float32),
    )
    state_now = attend_block(
        state_first, kv_local, my_block * token_rows, query_head_rows, query_place
    )

    def circle_step(step_num, carried):
        state_in, key_value_portion = carried
        key_value_portion = from_behind(key_value_portion, "ctx", 1)
        source = my_block - step_num
        state_out = lax.cond(
            source >= 0,
            lambda held: attend_block(
                held, key_value_portion, source * token_rows, query_head_rows, query_place
            ),
            lambda held: held,
            state_in,
        )
        return (state_out, key_value_portion)

    state_now, kv_last = lax.fori_loop(1, ctx_count, circle_step, (state_now, kv_local))
    row_top, row_total, accum = state_now
    attention = (
        (accum / row_total[..., None])
        .transpose(2, 0, 1, 3)
        .reshape(token_rows, QUERY_HEAD_COUNT * HEAD_SIZE)
        .astype(jnp.bfloat16)
    )
    all_rows = lax.all_gather(out_weight, "ctx", axis=0, tiled=True)
    projected = jnp.dot(
        attention,
        lax.all_gather(all_rows, "exp", axis=1, tiled=True),
        preferred_element_type=jnp.float32,
    )
    attn_resid = (resid[0].astype(jnp.float32) + projected).astype(jnp.bfloat16)
    resid_wide = attn_resid.astype(jnp.float32)
    scale_row = lax.rsqrt(jnp.mean(resid_wide * resid_wide, axis=-1, keepdims=True) + norm_eps)
    normed = (resid_wide * scale_row * norm_gain).astype(jnp.bfloat16)
    route_list = route_ids[0]
    local_experts = expert_gate.shape[0]
    expert_total = local_experts * exp_count
    expert_range = jnp.arange(expert_total, dtype=jnp.int32)
    expert_hits = jnp.sum(
        (route_list[:, :, None] == expert_range[None, None, :]).astype(jnp.int32), axis=1
    )
    earlier_hits = jnp.cumsum(expert_hits, axis=0) - expert_hits
    slot_index = jnp.take_along_axis(earlier_hits, route_list, axis=1)
    flat_index = route_list * CAP + slot_index
    token_range = jnp.arange(token_rows, dtype=jnp.int32)
    slot_token = jnp.full((expert_total * CAP,), token_rows, jnp.int32)
    slot_token = slot_token.at[flat_index.reshape(-1)].set(jnp.repeat(token_range, TOPK))
    normed_padded = jnp.concatenate([normed, jnp.zeros((1, normed.shape[1]), jnp.bfloat16)], axis=0)
    outgoing = normed_padded[slot_token].reshape(exp_count, local_experts, CAP, normed.shape[1])
    finished = experts_apply(
        lax.all_to_all(outgoing, "exp", split_axis=0, concat_axis=0, tiled=True),
        expert_gate,
        expert_up,
        expert_down,
    )
    returned_rows = lax.all_to_all(finished, "exp", split_axis=0, concat_axis=0, tiled=True)
    flat_out = returned_rows.reshape(expert_total * CAP, normed.shape[1])
    gate_rows = route_gates[0]
    shares = gate_rows / jnp.sum(gate_rows, axis=-1, keepdims=True)
    combined = resid_wide
    for column in range(TOPK):
        combined = combined + shares[:, column : column + 1] * flat_out[
            flat_index[:, column]
        ].astype(jnp.float32)
    layer_out = combined.astype(jnp.bfloat16)
    return (attn_resid[None], layer_out[None])


def solution(mesh):
    in_specs = (
        P("exp", "ctx", None),
        P("exp", "ctx", None),
        P("exp", "ctx", None),
        P("exp", "ctx", None),
        P("ctx", "exp"),
        P(),
        P("exp", None, None),
        P("exp", None, None),
        P("exp", None, None),
        P("exp", "ctx", None),
        P("exp", "ctx", None),
    )
    out_specs = (P("exp", "ctx", None), P("exp", "ctx", None))
    return jax.shard_map(local, mesh=mesh, in_specs=in_specs, out_specs=out_specs, check_vma=False)
```

profile of v0, /device:TPU:2, one launch (start us, length us, event | category | flops | bytes accessed | tf_op | source)
XLA Modules:
  0.0 518.5 jit_solution(5138913355031409357)
XLA Ops:
  8.0 42.1 %all-gather.3.cloned.1.call-done = bf16[4096,128]{1,0:T(8,128)(2,1)} async-done(((bf16[512,128]{1,0:T(8,128)(2,1)}), bf16[4096,128]{1,0:T(8,128)(2,1)}) %all-gather.3.cloned.1.call-update) | async-done | bytes 1048592 | tf_op jit(solution)/shard_map/all_gather | solution.py:108
  51.0 1.0 copy.78
  53.0 1.0 copy.79
  57.3 1.2 convolution_add_fusion.1
  58.5 118.7 %while.20 = (s32[]{:T(128)}, f32[4,8,128]{2,1,0:T(8,128)S(1)}, f32[4,8,128]{2,1,0:T(8,128)S(1)}, f32[4,8,128,128]{3,2,1,0:T(8,128)S(1)}, bf16[2,128,512]{1,2,0:T...) while((s32[]{:T(128)}, f32[4,8,128]{2,1,0:T(8,128)S(1)}, ...), condition=%wide.region_7.8_spmd.clone, body=%wide.region_2.7_spmd.clone.sunk | while | flops 276324608 | bytes 14224691 | solution.py:100
  58.5 1.9 collective-permute-start
  60.4 14.1 %collective-permute-done = bf16[2,128,512]{1,2,0:T(8,128)(2,1)S(1)} collective-permute-done((bf16[2,128,512]{1,2,0:T(8,128)(2,1)}, bf16[2,128,512]{1,2,0:T(8,128)(2,1)S(1)}, u32[]{:S(2)}, u32[]{:S(2)}) %collective-permute-start) | collective-permute-done | bytes 262176 | tf_op jit(solution)/shard_map/while/body/eval_jaxpr/ppermute | solution.py:20
  74.5 2.7 conditional.3
  75.7 1.4 multiply_add_fusion
  77.9 1.9 collective-permute-start
  79.8 8.6 %collective-permute-done = bf16[2,128,512]{1,2,0:T(8,128)(2,1)S(1)} collective-permute-done((bf16[2,128,512]{1,2,0:T(8,128)(2,1)}, bf16[2,128,512]{1,2,0:T(8,128)(2,1)S(1)}, u32[]{:S(2)}, u32[]{:S(2)}) %collective-permute-start) | collective-permute-done | bytes 262176 | tf_op jit(solution)/shard_map/while/body/eval_jaxpr/ppermute | solution.py:20
  88.5 2.7 conditional.3
  89.7 1.4 multiply_add_fusion
  91.9 1.9 collective-permute-start
  93.8 8.6 %collective-permute-done = bf16[2,128,512]{1,2,0:T(8,128)(2,1)S(1)} collective-permute-done((bf16[2,128,512]{1,2,0:T(8,128)(2,1)}, bf16[2,128,512]{1,2,0:T(8,128)(2,1)S(1)}, u32[]{:S(2)}, u32[]{:S(2)}) %collective-permute-start) | collective-permute-done | bytes 262176 | tf_op jit(solution)/shard_map/while/body/eval_jaxpr/ppermute | solution.py:20
  102.4 2.7 conditional.3
  103.7 1.4 multiply_add_fusion
  105.8 1.9 collective-permute-start
  107.8 15.8 %collective-permute-done = bf16[2,128,512]{1,2,0:T(8,128)(2,1)S(1)} collective-permute-done((bf16[2,128,512]{1,2,0:T(8,128)(2,1)}, bf16[2,128,512]{1,2,0:T(8,128)(2,1)S(1)}, u32[]{:S(2)}, u32[]{:S(2)}) %collective-permute-start) | collective-permute-done | bytes 262176 | tf_op jit(solution)/shard_map/while/body/eval_jaxpr/ppermute | solution.py:20
  123.6 2.7 conditional.3
  124.9 1.4 multiply_add_fusion
  127.0 1.9 collective-permute-start
  128.9 17.0 %collective-permute-done = bf16[2,128,512]{1,2,0:T(8,128)(2,1)S(1)} collective-permute-done((bf16[2,128,512]{1,2,0:T(8,128)(2,1)}, bf16[2,128,512]{1,2,0:T(8,128)(2,1)S(1)}, u32[]{:S(2)}, u32[]{:S(2)}) %collective-permute-start) | collective-permute-done | bytes 262176 | tf_op jit(solution)/shard_map/while/body/eval_jaxpr/ppermute | solution.py:20
  146.6 1.9 collective-permute-start
  148.5 16.7 %collective-permute-done = bf16[2,128,512]{1,2,0:T(8,128)(2,1)S(1)} collective-permute-done((bf16[2,128,512]{1,2,0:T(8,128)(2,1)}, bf16[2,128,512]{1,2,0:T(8,128)(2,1)S(1)}, u32[]{:S(2)}, u32[]{:S(2)}) %collective-permute-start) | collective-permute-done | bytes 262176 | tf_op jit(solution)/shard_map/while/body/eval_jaxpr/ppermute | solution.py:20
  165.9 1.9 collective-permute-start
  167.8 8.6 %collective-permute-done = bf16[2,128,512]{1,2,0:T(8,128)(2,1)S(1)} collective-permute-done((bf16[2,128,512]{1,2,0:T(8,128)(2,1)}, bf16[2,128,512]{1,2,0:T(8,128)(2,1)S(1)}, u32[]{:S(2)}, u32[]{:S(2)}) %collective-permute-start) | collective-permute-done | bytes 262176 | tf_op jit(solution)/shard_map/while/body/eval_jaxpr/ppermute | solution.py:20
  177.2 1.9 copy.81
  179.9 7.1 %gather_fusion.9 = s32[1024]{0:T(1024)S(1)} fusion(s32[128,32]{1,0:T(8,128)S(1)} %sub.39, s32[1024]{0:T(1024)S(1)} %reshape.236), kind=kCustom, calls=%fused_computation.9 | custom fusion | bytes 16384 | tf_op jit(solution)/shard_map/jit(take_along_axis)/gather | solution.py:126
  187.0 4.3 scatter_custom_fusion
  191.7 8.3 %fusion.35 = (f32[128]{0:T(128)S(1)}, bf16[128,2048]{1,0:T(8,128)(2,1)S(1)}) fusion(bf16[128,4096]{0,1:T(8,128)(2,1)S(1)} %bitcast.127, bf16[4096,2048]{1,0:T(8,128)(2,1)} %all-gather.5.cloned.1.call-done, bf16[1,128,2048]{2,1,0:T(8,128)(2,1)} %param.18), kind=kOutput, calls=%fused_computation.60 | convolution fusion | flops 2149056512 | bytes 18874880 | tf_op jit(solution)/shard_map/dot_general | solution.py:109
  200.2 11.0 %gather_fusion = bf16[2048,2048]{1,0:T(8,128)(2,1)} fusion(bf16[129,2048]{1,0:T(8,128)(2,1)S(1)} %concatenate.3, s32[2048]{0:T(1024)S(1)} %fusion.64), kind=kCustom, calls=%fused_computation | custom fusion | bytes 16785408 | tf_op jit(solution)/shard_map/gather | solution.py:132
  211.2 103.6 %all_to_all.10 = bf16[16,2,64,2048]{3,2,1,0:T(8,128)(2,1)S(1)} all-to-all(bf16[16,2,64,2048]{3,2,1,0:T(8,128)(2,1)} %bitcast.122), channel_id=1, replica_groups=mesh['ctx'=8,'exp'=16] {'exp'}, dimensions={0} | all-to-all | bytes 16777216 | tf_op jit(solution)/shard_map/all_to_all | solution.py:134
  314.8 10.6 %fusion.14 = f32[2,16,64,768]{3,2,1,0:T(8,128)} fusion(bf16[16,2,64,2048]{3,2,1,0:T(8,128)(2,1)S(1)} %all_to_all.10, bf16[2,2048,768]{2,1,0:T(8,128)(2,1)} %param.22), kind=kOutput, calls=%fused_computation.32 | convolution fusion | flops 6442450944 | bytes 20971520 | tf_op jit(solution)/shard_map/secd,edf->secf/dot_general | solution.py:49
  325.5 8.5 %fusion.16 = f32[2,16,64,768]{3,2,1,0:T(8,128)} fusion(bf16[16,2,64,2048]{3,2,1,0:T(8,128)(2,1)S(1)} %all_to_all.10, bf16[2,2048,768]{2,1,0:T(8,128)(2,1)S(1)} %bitcast.135), kind=kOutput, calls=%fused_computation.34 | convolution fusion | flops 6442450944 | bytes 20971520 | tf_op jit(solution)/shard_map/secd,edf->secf/dot_general | solution.py:46
  333.9 14.5 %convert_bitcast_fusion = bf16[16,2,64,2048]{3,2,0,1:T(8,128)(2,1)} fusion(bf16[2,768,2048]{2,1,0:T(8,128)(2,1)} %param.23, f32[2,16,64,768]{3,2,1,0:T(8,128)} %fusion.14, f32[2,16,64,768]{3,2,1,0:T(8,128)} %fusion.16), kind=kOutput, calls=%fused_computation.31 | convolution fusion | flops 6456082432 | bytes 27262976 | tf_op jit(solution)/shard_map/secf,efd->secd/dot_general | solution.py:51
  348.5 8.3 %copy.90 = bf16[16,2,64,2048]{3,2,1,0:T(8,128)(2,1)} copy(bf16[16,2,64,2048]{3,2,0,1:T(8,128)(2,1)} %convert_bitcast_fusion) | data formatting | bytes 16777216 | tf_op jit(solution)/shard_map/convert_element_type | solution.py:53
  356.7 5.0 all-to-all-start.1
  362.4 96.0 %all-to-all-done.1 = bf16[16,2,64,2048]{3,2,1,0:T(8,128)(2,1)} async-done(((bf16[16,2,64,2048]{3,2,1,0:T(8,128)(2,1)}), bf16[16,2,64,2048]{3,2,1,0:T(8,128)(2,1)}, u32[]{:S(2)}, u32[]{:S(2)}) %all-to-all-start.1) | async-done | bytes 8388640 | tf_op jit(solution)/shard_map/all_to_all | solution.py:139
  458.4 5.9 %gather_fusion.1 = bf16[128,2048]{1,0:T(8,128)(2,1)S(1)} fusion(bf16[2048,2048]{1,0:T(8,128)(2,1)} %bitcast.30, s32[1024]{0:T(1024)S(1)} %get-tuple-element.290), kind=kCustom, calls=%fused_computation.1 | custom fusion | bytes 1049088 | tf_op jit(solution)/shard_map/gather | solution.py:145
  464.3 5.9 %gather_fusion.2 = bf16[128,2048]{1,0:T(8,128)(2,1)S(1)} fusion(bf16[2048,2048]{1,0:T(8,128)(2,1)} %bitcast.30, s32[1024]{0:T(1024)S(1)} %get-tuple-element.289), kind=kCustom, calls=%fused_computation.2 | custom fusion | bytes 1049088 | tf_op jit(solution)/shard_map/gather | solution.py:145
  470.2 5.9 %gather_fusion.3 = bf16[128,2048]{1,0:T(8,128)(2,1)S(1)} fusion(bf16[2048,2048]{1,0:T(8,128)(2,1)} %bitcast.30, s32[1024]{0:T(1024)S(1)} %get-tuple-element.288), kind=kCustom, calls=%fused_computation.3 | custom fusion | bytes 1049088 | tf_op jit(solution)/shard_map/gather | solution.py:145
  476.1 5.9 %gather_fusion.4 = bf16[128,2048]{1,0:T(8,128)(2,1)S(1)} fusion(bf16[2048,2048]{1,0:T(8,128)(2,1)} %bitcast.30, s32[1024]{0:T(1024)S(1)} %get-tuple-element.287), kind=kCustom, calls=%fused_computation.4 | custom fusion | bytes 1049088 | tf_op jit(solution)/shard_map/gather | solution.py:145
  482.0 5.9 %gather_fusion.5 = bf16[128,2048]{1,0:T(8,128)(2,1)S(1)} fusion(bf16[2048,2048]{1,0:T(8,128)(2,1)} %bitcast.30, s32[1024]{0:T(1024)S(1)} %get-tuple-element.286), kind=kCustom, calls=%fused_computation.5 | custom fusion | bytes 1049088 | tf_op jit(solution)/shard_map/gather | solution.py:145
  487.9 7.0 %gather_fusion.6 = bf16[128,2048]{1,0:T(8,128)(2,1)} fusion(bf16[2048,2048]{1,0:T(8,128)(2,1)} %bitcast.30, s32[1024]{0:T(1024)S(1)} %get-tuple-element.285), kind=kCustom, calls=%fused_computation.6 | custom fusion | bytes 1049088 | tf_op jit(solution)/shard_map/gather | solution.py:145
  494.9 6.7 %gather_fusion.7 = bf16[128,2048]{1,0:T(8,128)(2,1)} fusion(bf16[2048,2048]{1,0:T(8,128)(2,1)} %bitcast.30, s32[1024]{0:T(1024)S(1)} %get-tuple-element.284), kind=kCustom, calls=%fused_computation.7 | custom fusion | bytes 1049088 | tf_op jit(solution)/shard_map/gather | solution.py:145
  501.6 6.7 %gather_fusion.8 = bf16[128,2048]{1,0:T(8,128)(2,1)} fusion(bf16[2048,2048]{1,0:T(8,128)(2,1)} %bitcast.30, s32[1024]{0:T(1024)S(1)} %get-tuple-element.283), kind=kCustom, calls=%fused_computation.8 | custom fusion | bytes 1049088 | tf_op jit(solution)/shard_map/gather | solution.py:145
  508.3 3.1 fusion.51
  (109 shorter events, 17.5 us)
Async XLA Ops:
  7.2 46.9 %copy-start.2 = (bf16[1,128,4096]{2,1,0:T(8,128)(2,1)S(1)}, bf16[1,128,4096]{2,1,0:T(8,128)(2,1)}, u32[]{:S(2)}) copy-start(bf16[1,128,4096]{2,1,0:T(8,128)(2,1)} %param.15) | copy-start | bytes 3145732
  7.2 42.9 %all-gather.3.cloned.1.call-start = ((), (), s32[]{:S(2)}) async-start(), calls=%async_computation.2 | async-start | bytes 1179648 | tf_op jit(solution)/shard_map/all_gather | solution.py:108
  7.9 183.7 %all-gather.5.cloned.1.call-start = ((), (), s32[]{:S(2)}) async-start(), calls=%async_computation.3 | async-start | bytes 17825792 | tf_op jit(solution)/shard_map/all_gather | solution.py:111
  58.5 16.0 %collective-permute-start = (bf16[2,128,512]{1,2,0:T(8,128)(2,1)}, bf16[2,128,512]{1,2,0:T(8,128)(2,1)S(1)}, u32[]{:S(2)}, u32[]{:S(2)}) collective-permute-start(bf16[2,128,512]{1,2,0:T(8,128)(2,1)} %get-tuple-element.366), channel_id=1, source_target_pairs={{0,16},{16,32},{32,48},{48,64},{64,80},{80,96},{96,112},{1,17},{17... | collective-permute-start | bytes 786440 | tf_op jit(solution)/shard_map/while/body/eval_jaxpr/ppermute | solution.py:20
  77.9 10.6 %collective-permute-start = (bf16[2,128,512]{1,2,0:T(8,128)(2,1)}, bf16[2,128,512]{1,2,0:T(8,128)(2,1)S(1)}, u32[]{:S(2)}, u32[]{:S(2)}) collective-permute-start(bf16[2,128,512]{1,2,0:T(8,128)(2,1)} %get-tuple-element.366), channel_id=1, source_target_pairs={{0,16},{16,32},{32,48},{48,64},{64,80},{80,96},{96,112},{1,17},{17... | collective-permute-start | bytes 786440 | tf_op jit(solution)/shard_map/while/body/eval_jaxpr/ppermute | solution.py:20
  91.9 10.6 %collective-permute-start = (bf16[2,128,512]{1,2,0:T(8,128)(2,1)}, bf16[2,128,512]{1,2,0:T(8,128)(2,1)S(1)}, u32[]{:S(2)}, u32[]{:S(2)}) collective-permute-start(bf16[2,128,512]{1,2,0:T(8,128)(2,1)} %get-tuple-element.366), channel_id=1, source_target_pairs={{0,16},{16,32},{32,48},{48,64},{64,80},{80,96},{96,112},{1,17},{17... | collective-permute-start | bytes 786440 | tf_op jit(solution)/shard_map/while/body/eval_jaxpr/ppermute | solution.py:20
  105.8 17.8 %collective-permute-start = (bf16[2,128,512]{1,2,0:T(8,128)(2,1)}, bf16[2,128,512]{1,2,0:T(8,128)(2,1)S(1)}, u32[]{:S(2)}, u32[]{:S(2)}) collective-permute-start(bf16[2,128,512]{1,2,0:T(8,128)(2,1)} %get-tuple-element.366), channel_id=1, source_target_pairs={{0,16},{16,32},{32,48},{48,64},{64,80},{80,96},{96,112},{1,17},{17... | collective-permute-start | bytes 786440 | tf_op jit(solution)/shard_map/while/body/eval_jaxpr/ppermute | solution.py:20
  127.0 18.9 %collective-permute-start = (bf16[2,128,512]{1,2,0:T(8,128)(2,1)}, bf16[2,128,512]{1,2,0:T(8,128)(2,1)S(1)}, u32[]{:S(2)}, u32[]{:S(2)}) collective-permute-start(bf16[2,128,512]{1,2,0:T(8,128)(2,1)} %get-tuple-element.366), channel_id=1, source_target_pairs={{0,16},{16,32},{32,48},{48,64},{64,80},{80,96},{96,112},{1,17},{17... | collective-permute-start | bytes 786440 | tf_op jit(solution)/shard_map/while/body/eval_jaxpr/ppermute | solution.py:20
  146.6 18.6 %collective-permute-start = (bf16[2,128,512]{1,2,0:T(8,128)(2,1)}, bf16[2,128,512]{1,2,0:T(8,128)(2,1)S(1)}, u32[]{:S(2)}, u32[]{:S(2)}) collective-permute-start(bf16[2,128,512]{1,2,0:T(8,128)(2,1)} %get-tuple-element.366), channel_id=1, source_target_pairs={{0,16},{16,32},{32,48},{48,64},{64,80},{80,96},{96,112},{1,17},{17... | collective-permute-start | bytes 786440 | tf_op jit(solution)/shard_map/while/body/eval_jaxpr/ppermute | solution.py:20
  165.9 10.6 %collective-permute-start = (bf16[2,128,512]{1,2,0:T(8,128)(2,1)}, bf16[2,128,512]{1,2,0:T(8,128)(2,1)S(1)}, u32[]{:S(2)}, u32[]{:S(2)}) collective-permute-start(bf16[2,128,512]{1,2,0:T(8,128)(2,1)} %get-tuple-element.366), channel_id=1, source_target_pairs={{0,16},{16,32},{32,48},{48,64},{64,80},{80,96},{96,112},{1,17},{17... | collective-permute-start | bytes 786440 | tf_op jit(solution)/shard_map/while/body/eval_jaxpr/ppermute | solution.py:20
  177.2 1.9 copy-start.3
  179.9 11.5 %copy-start = (f32[4,8,128,128]{2,3,1,0:T(8,128)S(1)}, f32[4,8,128,128]{2,3,1,0:T(8,128)}, u32[]{:S(2)}) copy-start(f32[4,8,128,128]{2,3,1,0:T(8,128)} %copy.81) | copy-start | bytes 6291460
  191.6 8.3 %copy-start.5 = (f32[2048]{0:T(1024)S(1)}, f32[2048]{0:T(1024)}, u32[]{:S(2)}) copy-start(f32[2048]{0:T(1024)} %param.20) | copy-start | bytes 24580
  200.0 308.4 %copy-start.1 = (bf16[128,2048]{1,0:T(8,128)(2,1)}, bf16[128,2048]{1,0:T(8,128)(2,1)S(1)}, u32[]{:S(2)}) copy-start(bf16[128,2048]{1,0:T(8,128)(2,1)S(1)} %get-tuple-element.282) | copy-start | bytes 1572868
  211.2 114.2 %slice-start = ((s8[6291456]{0:T(1024)(128)(4,1)}), s8[4194304]{0:T(1024)(128)(4,1)S(1)}, s32[]{:S(2)}) async-start(s8[6291456]{0:T(1024)(128)(4,1)} %bitcast.134), calls=%async_computation.4 | async-start | bytes 8388608
  314.8 10.6 %slice-start.1 = ((s8[6291456]{0:T(1024)(128)(4,1)}), s8[2097152]{0:T(1024)(128)(4,1)S(1)}, s32[]{:S(2)}) async-start(s8[6291456]{0:T(1024)(128)(4,1)} %bitcast.134), calls=%async_computation.5 | async-start | bytes 4194304
  356.7 5.1 copy-start.4
  356.7 101.6 %all-to-all-start.1 = ((bf16[16,2,64,2048]{3,2,1,0:T(8,128)(2,1)}), bf16[16,2,64,2048]{3,2,1,0:T(8,128)(2,1)}, u32[]{:S(2)}, u32[]{:S(2)}) async-start(bf16[16,2,64,2048]{3,2,1,0:T(8,128)(2,1)} %copy.90), calls=%async_computation.1 | async-start | bytes 16777216 | tf_op jit(solution)/shard_map/all_to_all | solution.py:139
Sparse Core Ops, SparseCore 0:
  9.7 40.3 all-gather.2
  52.4 122.8 all-gather.4
where the time goes:
time: 528 us; the launch traced here: 518 us
  waiting for transfers between devices  228 us (43%)
  blocking collectives  104 us (20%)
  local copies, waits for them, and re-layouts  93.5 us (18%)
  matrix products  51.3 us (10%)
  starting transfers between devices  18.5 us (4%)
  between operations  14.6 us (3%)
  other arithmetic  8.29 us (2%)
    all_to_all x1, blocking collectives, local(): lax.all_to_all(outgoing, 'exp', split_axis=0, concat_axis=0, tiled=True)  104 us
    all_to_all x1, waiting for transfers between devices, local(): lax.all_to_all(finished, 'exp', split_axis=0, concat_axis=0, tiled=True)  96 us
    ppermute x7, waiting for transfers between devices, from_behind(): return lax.ppermute(shard, axis, pairs)  89.5 us
    gather x8, local copies, waits for them, and re-layouts, local(): flat_out[flat_index[:, column]].astype(jnp.float32)  49.9 us
    all_gather x1, waiting for transfers between devices, local(): all_rows = lax.all_gather(out_weight, 'ctx', axis=0, tiled=True)  42.1 us
    dot_general x1, matrix products, experts_apply(): jnp.einsum('secf,efd->secd', activated, down_local, preferred_element_typ...  14.5 us
    ppermute x7, starting transfers between devices, from_behind(): return lax.ppermute(shard, axis, pairs)  13.4 us
    gather x1, local copies, waits for them, and re-layouts, local(): normed_padded[slot_token]  11 us
  transfers between devices with their start and end apart: 10, of which 9 were waited for; matrix products, arithmetic and copies ran while one was open for 7% of the time, Pallas kernels for 0%

commit v1 on v0

--- a/solution.py
+++ b/solution.py
@@ -1,6 +1,10 @@
+import functools
+
 import jax
 import jax.numpy as jnp
 from jax import lax
+from jax.experimental import pallas as pl
+from jax.experimental.pallas import tpu as pltpu
 from jax.sharding import PartitionSpec as P
 
 QUERY_HEAD_COUNT = 32
@@ -8,10 +12,356 @@
 HEAD_SIZE = 128
 TOPK = 8
 CAP = 64
-
+TOK = 128
+D = 2048
+FF = 768
+EXPERTS = 32
+MESH = pl.DeviceIdType.MESH
 
 norm_eps = 1e-06
 mask_fill_value = -1e30
+
+RELATIONS = ((0, 0), (3, 0), (1, 0), (0, 1), (2, 0), (3, 1), (1, 1), (2, 1))
+PAIRS = ((0, 3), (1, 2), (4, 7), (5, 6))
+
+
+def moe_kernel(
+    normed_ref,
+    resid_ref,
+    share_ref,
+    gate_hbm,
+    up_hbm,
+    down_hbm,
+    out_ref,
+    gate_w,
+    up_w,
+    down_w,
+    blocks,
+    parts,
+    sib_parts,
+    half_in,
+    full_in,
+    far_in,
+    hop_in,
+    slots_in,
+    slots_out,
+    act,
+    weight_sem,
+    ag_send,
+    ag_recv,
+    sib_send,
+    sib_recv,
+    part_send,
+    part_recv,
+    rs_send,
+    rs_recv,
+):
+    me = lax.axis_index("exp")
+    z, xh, core = me // 4, lax.rem(me // 2, 2), lax.rem(me, 2)
+
+    def block_of(relation, which):
+        dz, dx = RELATIONS[relation]
+        return lax.rem(z + dz, 4) * 4 + lax.rem(xh + dx, 2) * 2 + which
+
+    other = 1 - core
+    sibling = me + 1 - 2 * core
+    z_up, z_down, x_over = block_of(2, core), block_of(1, core), block_of(3, core)
+
+    loads = []
+    for number, (src, dst) in enumerate(((gate_hbm, gate_w), (up_hbm, up_w), (down_hbm, down_w))):
+        loads.append(pltpu.make_async_copy(src, dst, weight_sem.at[number]))
+        loads[-1].start()
+    blocks[me] = normed_ref[...]
+
+    barrier = pltpu.get_barrier_semaphore()
+    for peer in (sibling, z_up, z_down, x_over):
+        pl.semaphore_signal(barrier, inc=1, device_id={"exp": peer}, device_id_type=MESH)
+    pl.semaphore_wait(barrier, 4)
+
+    def send(src, dst, sems, number, peer):
+        return pltpu.make_async_remote_copy(
+            src_ref=src,
+            dst_ref=dst,
+            send_sem=sems[0].at[number],
+            recv_sem=sems[1].at[number],
+            device_id={"exp": peer},
+            device_id_type=MESH,
+        )
+
+    ag = (ag_send, ag_recv)
+    sib = (sib_send, sib_recv)
+    part = (part_send, part_recv)
+    rs = (rs_send, rs_recv)
+    low, high = pl.ds(0, CAP), pl.ds(CAP, CAP)
+
+    def whole(relation):
+        return blocks.at[block_of(relation, core)]
+
+    def half(relation, rows):
+        return blocks.at[block_of(relation, core), rows]
+
+    ag_out = (
+        send(whole(0), whole(0), ag, 0, z_up),
+        send(whole(0), whole(0), ag, 1, z_down),
+        send(whole(0), whole(0), ag, 2, x_over),
+        send(half(1, low), half(1, low), ag, 3, z_up),
+        send(half(2, high), half(2, high), ag, 4, z_down),
+        send(whole(3), whole(3), ag, 5, z_up),
+        send(whole(3), whole(3), ag, 6, z_down),
+        send(whole(4), whole(4), ag, 7, x_over),
+    )
+    ag_in = (
+        send(whole(1), whole(1), ag, 0, z_up),
+        send(whole(2), whole(2), ag, 1, z_down),
+        send(whole(3), whole(3), ag, 2, x_over),
+        send(half(4, low), half(4, low), ag, 3, z_up),
+        send(half(4, high), half(4, high), ag, 4, z_down),
+        send(whole(5), whole(5), ag, 5, z_up),
+        send(whole(6), whole(6), ag, 6, z_down),
+        send(whole(7), whole(7), ag, 7, x_over),
+    )
+    sib_out = [send(whole(k), whole(k), sib, k, sibling) for k in range(8)]
+    sib_in = []
+    for k in range(8):
+        arriving = blocks.at[block_of(k, other)]
+        sib_in.append(send(arriving, arriving, sib, k, sibling))
+
+    for number in (0, 1, 2):
+        ag_out[number].start()
+    sib_out[0].start()
+    for load in loads:
+        load.wait()
+
+    lane = lax.broadcasted_iota(jnp.int32, (TOK, TOK), 1)
+    row = lax.broadcasted_iota(jnp.int32, (TOK, TOK), 0)
+    up_to = (row <= lane).astype(jnp.bfloat16)
+    slot_of_row = lax.rem(row, CAP).astype(jnp.float32)
+
+    def part_copy(chip):
+        return send(parts.at[chip * 2 + other], sib_parts.at[chip], part, chip, sibling)
+
+    def selection(block):
+        both = share_ref[block]
+        chosen = both > 0.0
+        count = jnp.dot(
+            chosen.astype(jnp.bfloat16), up_to, preferred_element_type=jnp.float32
+        )
+        place = jnp.where(chosen, count - 1.0, -1.0)
+        place_rows = jnp.concatenate(
+            [jnp.broadcast_to(place[j : j + 1], (CAP, TOK)) for j in range(2)], axis=0
+        )
+        share_rows = jnp.concatenate(
+            [jnp.broadcast_to(both[j : j + 1], (CAP, TOK)) for j in range(2)], axis=0
+        )
+        picked = place_rows == slot_of_row
+        slot_share = jnp.sum(jnp.where(picked, share_rows, 0.0), axis=1, keepdims=True)
+        return picked.astype(jnp.float32), slot_share
+
+    def step(number, carry):
+        @pl.when(number == 0)
+        def _():
+            ag_in[0].wait_recv()
+            ag_out[3].start()
+            sib_out[1].start()
+            ag_in[1].wait_recv()
+            ag_out[4].start()
+            sib_out[2].start()
+            ag_in[2].wait_recv()
+            ag_out[5].start()
+            ag_out[6].start()
+            sib_out[3].start()
+            sib_in[0].wait_recv()
+            sib_in[3].wait_recv()
+
+        @pl.when(number == 1)
+        def _():
+            ag_in[3].wait_recv()
+            ag_in[4].wait_recv()
+            ag_out[7].start()
+            sib_out[4].start()
+            sib_in[1].wait_recv()
+            sib_in[2].wait_recv()
+
+        @pl.when(number == 2)
+        def _():
+            ag_in[5].wait_recv()
+            sib_out[5].start()
+            ag_in[6].wait_recv()
+            sib_out[6].start()
+            ag_in[7].wait_recv()
+            sib_out[7].start()
+            sib_in[4].wait_recv()
+            sib_in[7].wait_recv()
+
+        @pl.when(number == 3)
+        def _():
+            sib_in[5].wait_recv()
+            sib_in[6].wait_recv()
+
+        def chip_at(which):
+            dz, dx = 0, 0
+            for k, pair in enumerate(PAIRS):
+                here = RELATIONS[pair[which]]
+                dz = jnp.where(number == k, here[0], dz)
+                dx = jnp.where(number == k, here[1], dx)
+            return lax.rem(z + dz, 4) * 2 + lax.rem(xh + dx, 2)
+
+        chips = (chip_at(0), chip_at(1))
+        sources = [chips[q // 2] * 2 + q % 2 for q in range(4)]
+        for q in range(4):
+            picked, _ = selection(sources[q])
+            found = jnp.dot(
+                picked.astype(jnp.bfloat16),
+                blocks[sources[q]],
+                preferred_element_type=jnp.float32,
+            ).astype(jnp.bfloat16)
+            for j in range(2):
+                slots_in[j, q * CAP : (q + 1) * CAP] = found[j * CAP : (j + 1) * CAP]
+
+        def expert(j, carry):
+            for n in range(3):
+                cols = slice(n * 256, (n + 1) * 256)
+                gate_part = jnp.dot(
+                    slots_in[j], gate_w[j, :, cols], preferred_element_type=jnp.float32
+                )
+                up_part = jnp.dot(
+                    slots_in[j], up_w[j, :, cols], preferred_element_type=jnp.float32
+                )
+                act[:, cols] = (gate_part / (1.0 + jnp.exp(-gate_part)) * up_part).astype(
+                    jnp.bfloat16
+                )
+            for n in range(4):
+                cols = slice(n * 512, (n + 1) * 512)
+                result = jnp.dot(act[...], down_w[j, :, cols], preferred_element_type=jnp.float32)
+                for q in range(4):
+                    slots_out[q, pl.ds(pl.multiple_of(j * CAP, CAP), CAP), cols] = result[
+                        q * CAP : (q + 1) * CAP
+                    ].astype(jnp.bfloat16)
+            return carry
+
+        lax.fori_loop(0, 2, expert, 0)
+        for q in range(4):
+            picked, slot_share = selection(sources[q])
+            scaled = (slots_out[q].astype(jnp.float32) * slot_share).astype(jnp.bfloat16)
+            parts[sources[q]] = jnp.dot(
+                picked.T.astype(jnp.bfloat16), scaled, preferred_element_type=jnp.float32
+            ).astype(jnp.bfloat16)
+            if q % 2:
+                part_copy(chips[q // 2]).start()
+        return carry
+
+    lax.fori_loop(0, 4, step, 0)
+
+    def chip_sum(relation):
+        dz, dx = RELATIONS[relation]
+        chip = lax.rem(z + dz, 4) * 2 + lax.rem(xh + dx, 2)
+        pltpu.make_async_remote_copy(
+            src_ref=parts.at[chip * 2 + other],
+            dst_ref=sib_parts.at[chip],
+            send_sem=part_send.at[chip],
+            recv_sem=part_recv.at[chip],
+            device_id={"exp": sibling},
+            device_id_type=MESH,
+        ).wait_recv()
+        add_into(chip * 2 + core, slice(None), sib_parts.at[chip])
+
+    def add_into(block, rows, extra):
+        parts[block, rows] = (
+            parts[block, rows].astype(jnp.float32) + extra[...].astype(jnp.float32)
+        ).astype(jnp.bfloat16)
+
+    def part_of(relation):
+        return parts.at[block_of(relation, core)]
+
+    chip_sum(7)
+    rs_out = [send(part_of(7), hop_in, rs, 0, x_over)]
+    rs_out[0].start()
+    chip_sum(5)
+    rs_out.append(send(part_of(5), full_in.at[2], rs, 1, z_down))
+    rs_out[1].start()
+    chip_sum(6)
+    rs_out.append(send(part_of(6), full_in.at[3], rs, 2, z_up))
+    rs_out[2].start()
+    chip_sum(4)
+    rs_out[0].wait_recv()
+    add_into(block_of(4, core), slice(None), hop_in)
+    rs_out.append(
+        send(parts.at[block_of(4, core), low], half_in.at[0], rs, 3, z_down)
+    )
+    rs_out[3].start()
+    rs_out.append(send(parts.at[block_of(4, core), high], half_in.at[1], rs, 4, z_up))
+    rs_out[4].start()
+    chip_sum(3)
+    chip_sum(1)
+    chip_sum(2)
+    chip_sum(0)
+    rs_out[1].wait_recv()
+    add_into(block_of(3, core), slice(None), full_in.at[2])
+    rs_out[2].wait_recv()
+    add_into(block_of(3, core), slice(None), full_in.at[3])
+    rs_out.append(send(part_of(3), far_in, rs, 5, x_over))
+    rs_out[5].start()
+    rs_out[3].wait_recv()
+    add_into(block_of(1, core), slice(0, CAP), half_in.at[0])
+    rs_out.append(send(part_of(1), full_in.at[0], rs, 6, z_down))
+    rs_out[6].start()
+    rs_out[4].wait_recv()
+    add_into(block_of(2, core), slice(CAP, TOK), half_in.at[1])
+    rs_out.append(send(part_of(2), full_in.at[1], rs, 7, z_up))
+    rs_out[7].start()
+
+    rs_out[6].wait_recv()
+    rs_out[7].wait_recv()
+    rs_out[5].wait_recv()
+    total = resid_ref[...].astype(jnp.float32) + parts[me].astype(jnp.float32)
+    for extra in (full_in.at[0], full_in.at[1], far_in):
+        total = total + extra[...].astype(jnp.float32)
+    out_ref[...] = total.astype(jnp.bfloat16)
+
+    for copy in (*ag_out, *sib_out, *rs_out):
+        copy.wait_send()
+    for chip in range(8):
+        part_copy(chip).wait_send()
+
+
+def moe(normed, attn_resid, shares, expert_gate, expert_up, expert_down):
+    vmem = pl.BlockSpec(memory_space=pltpu.VMEM)
+    hbm = pl.BlockSpec(memory_space=pl.ANY)
+    dma = pltpu.SemaphoreType.DMA
+    bf16 = jnp.bfloat16
+    return pl.pallas_call(
+        moe_kernel,
+        out_shape=jax.ShapeDtypeStruct((TOK, D), bf16),
+        in_specs=[vmem, vmem, vmem, hbm, hbm, hbm],
+        out_specs=vmem,
+        scratch_shapes=[
+            pltpu.VMEM((2, D, FF), bf16),
+            pltpu.VMEM((2, D, FF), bf16),
+            pltpu.VMEM((2, FF, D), bf16),
+            pltpu.VMEM((16, TOK, D), bf16),
+            pltpu.VMEM((16, TOK, D), bf16),
+            pltpu.VMEM((8, TOK, D), bf16),
+            pltpu.VMEM((2, CAP, D), bf16),
+            pltpu.VMEM((4, TOK, D), bf16),
+            pltpu.VMEM((TOK, D), bf16),
+            pltpu.VMEM((TOK, D), bf16),
+            pltpu.VMEM((2, 256, D), bf16),
+            pltpu.VMEM((4, TOK, D), bf16),
+            pltpu.VMEM((256, FF), bf16),
+            dma((3,)),
+            dma((8,)),
+            dma((8,)),
+            dma((8,)),
+            dma((8,)),
+            dma((8,)),
+            dma((8,)),
+            dma((8,)),
+            dma((8,)),
+        ],
+        compiler_params=pltpu.CompilerParams(
+            collective_id=1, has_side_effects=True, vmem_limit_bytes=60 << 20
+        ),
+    )(normed, attn_resid, shares, expert_gate, expert_up, expert_down)
 
 
 def from_behind(shard, axis, by):
@@ -40,17 +390,6 @@
         "ngtu,und->ngtd", weights, value_head_rows, preferred_element_type=jnp.float32
     )
     return (new_top, row_total, accum)
-
-
-def experts_apply(arrived, gate_local, up_local, down_local):
-    gate_part = jnp.einsum(
-        "secd,edf->secf", arrived, gate_local, preferred_element_type=jnp.float32
-    )
-    up_part = jnp.einsum("secd,edf->secf", arrived, up_local, preferred_element_type=jnp.float32)
-    activated = (jax.nn.silu(gate_part) * up_part).astype(jnp.bfloat16)
-    return jnp.einsum(
-        "secf,efd->secd", activated, down_local, preferred_element_type=jnp.float32
-    ).astype(jnp.bfloat16)
 
 
 def local(
@@ -115,37 +454,13 @@
     resid_wide = attn_resid.astype(jnp.float32)
     scale_row = lax.rsqrt(jnp.mean(resid_wide * resid_wide, axis=-1, keepdims=True) + norm_eps)
     normed = (resid_wide * scale_row * norm_gain).astype(jnp.bfloat16)
-    route_list = route_ids[0]
-    local_experts = expert_gate.shape[0]
-    expert_total = local_experts * exp_count
-    expert_range = jnp.arange(expert_total, dtype=jnp.int32)
-    expert_hits = jnp.sum(
-        (route_list[:, :, None] == expert_range[None, None, :]).astype(jnp.int32), axis=1
-    )
-    earlier_hits = jnp.cumsum(expert_hits, axis=0) - expert_hits
-    slot_index = jnp.take_along_axis(earlier_hits, route_list, axis=1)
-    flat_index = route_list * CAP + slot_index
-    token_range = jnp.arange(token_rows, dtype=jnp.int32)
-    slot_token = jnp.full((expert_total * CAP,), token_rows, jnp.int32)
-    slot_token = slot_token.at[flat_index.reshape(-1)].set(jnp.repeat(token_range, TOPK))
-    normed_padded = jnp.concatenate([normed, jnp.zeros((1, normed.shape[1]), jnp.bfloat16)], axis=0)
-    outgoing = normed_padded[slot_token].reshape(exp_count, local_experts, CAP, normed.shape[1])
-    finished = experts_apply(
-        lax.all_to_all(outgoing, "exp", split_axis=0, concat_axis=0, tiled=True),
-        expert_gate,
-        expert_up,
-        expert_down,
-    )
-    returned_rows = lax.all_to_all(finished, "exp", split_axis=0, concat_axis=0, tiled=True)
-    flat_out = returned_rows.reshape(expert_total * CAP, normed.shape[1])
     gate_rows = route_gates[0]
     shares = gate_rows / jnp.sum(gate_rows, axis=-1, keepdims=True)
-    combined = resid_wide
-    for column in range(TOPK):
-        combined = combined + shares[:, column : column + 1] * flat_out[
-            flat_index[:, column]
-        ].astype(jnp.float32)
-    layer_out = combined.astype(jnp.bfloat16)
+    hits = route_ids[0][:, :, None] == jnp.arange(EXPERTS, dtype=jnp.int32)[None, None, :]
+    dense = jnp.sum(jnp.where(hits, shares[:, :, None], 0.0), axis=1)
+    wanted = jnp.pad(dense.T.reshape(exp_count, 2, token_rows), ((0, 0), (0, 6), (0, 0)))
+    shares_here = lax.all_to_all(wanted, "exp", split_axis=0, concat_axis=0, tiled=True)
+    layer_out = moe(normed, attn_resid, shares_here, expert_gate, expert_up, expert_down)
     return (attn_resid[None], layer_out[None])
 
 

time: 528 us -> 307 us (0.58); the launches traced: 518 us -> 305 us
  blocking collectives: 104 us -> 0 us
  Pallas kernels: 0 us -> 95.5 us
  waiting for transfers between devices: 228 us -> 134 us
  local copies, waits for them, and re-layouts: 93.5 us -> 14.4 us
  matrix products: 51.3 us -> 17.7 us
    all_to_all x1 -> x0, blocking collectives: 104 us -> none  [local(): lax.all_to_all(outgoing, 'exp', split_axis=0, concat_axis=0, tiled=True)]
    all_to_all x1, waiting for transfers between devices: 96 us -> 0.01 us  [local(): lax.all_to_all(wanted, 'exp', split_axis=0, concat_axis=0, tiled=True)]
    pallas_call x0 -> x1, Pallas kernels: none -> 95.5 us  [moe(): pl.pallas_call(moe_kernel, out_shape=jax.ShapeDtypeStruct((TOK, D), bf16)...]
    gather x13 -> x0, local copies, waits for them, and re-layouts: 68.3 us -> none  [the longest x8 49.9 us: local(): flat_out[flat_index[:, column]].astype(jnp.float32)]
    dot_general x3 -> x0, matrix products: 33.6 us -> none  [the longest x1 14.5 us: experts_apply(): jnp.einsum('secf,efd->secd', activated, down_local, preferred_element_typ...]
    convert_element_type x1 -> x0, local copies, waits for them, and re-layouts: 8.25 us -> none  [experts_apply(): return jnp.einsum('secf,efd->secd', activated, down_local, preferred_elem...]
  transfers between devices with their start and end apart: 10 -> 10, of which waited for: 9 -> 8; matrix products, arithmetic and copies ran while one was open for 7% -> 13% of each run, Pallas kernels for 0% -> 0%
where the time goes in v1:
time: 307 us; the launch traced here: 305 us
  waiting for transfers between devices  134 us (44%)
  Pallas kernels  95.5 us (31%)
  starting transfers between devices  19.8 us (6%)
  matrix products  17.7 us (6%)
  local copies, waits for them, and re-layouts  14.4 us (5%)
  between operations  14.2 us (5%)
  other arithmetic  9.04 us (3%)
    pallas_call x1, Pallas kernels, moe(): pl.pallas_call(moe_kernel, out_shape=jax.ShapeDtypeStruct((TOK, D), bf16)...  95.5 us
    ppermute x7, waiting for transfers between devices, from_behind(): return lax.ppermute(shard, axis, pairs)  90.8 us
    all_gather x1, waiting for transfers between devices, local(): all_rows = lax.all_gather(out_weight, 'ctx', axis=0, tiled=True)  42.1 us
    ppermute x7, starting transfers between devices, from_behind(): return lax.ppermute(shard, axis, pairs)  13.4 us
    dot_general x1, matrix products, local(): jnp.dot(attention, lax.all_gather(all_rows, 'exp', axis=1, tiled=True), p...  8.23 us
    dot_general x5, matrix products, attend_block(): jnp.einsum('ngtu,und->ngtd', weights, value_head_rows, preferred_element_...  6.9 us
    all_to_all x1, starting transfers between devices, local(): lax.all_to_all(wanted, 'exp', split_axis=0, concat_axis=0, tiled=True)  6.34 us
  transfers between devices with their start and end apart: 10, of which 8 were waited for; matrix products, arithmetic and copies ran while one was open for 13% of the time, Pallas kernels for 0%

profile of v1, /device:TPU:2, one launch (start us, length us, event | category | flops | bytes accessed | tf_op | source)
XLA Modules:
  0.0 304.6 jit_solution(4843840594411465447)
XLA Ops:
  7.2 0.7 all-gather.3.cloned.1.call-update
  8.0 42.1 %all-gather.3.cloned.1.call-done = bf16[4096,128]{1,0:T(8,128)(2,1)} async-done(((bf16[512,128]{1,0:T(8,128)(2,1)}), bf16[4096,128]{1,0:T(8,128)(2,1)}) %all-gather.3.cloned.1.call-update) | async-done | bytes 1048592 | tf_op jit(solution)/shard_map/all_gather | solution.py:447
  50.1 0.7 reduce_sum.47
  50.8 0.7 bitcast_divide_fusion
  51.5 0.7 select_reduce_fusion
  52.8 6.3 %all-to-all-start = ((f32[16,8,128]{2,1,0:T(8,128)}), f32[16,8,128]{2,1,0:T(8,128)S(1)}, u32[]{:S(2)}, u32[]{:S(2)}) async-start(f32[16,8,128]{2,1,0:T(8,128)} %pad.4), calls=%async_computation | async-start | bytes 131072 | tf_op jit(solution)/shard_map/all_to_all | solution.py:462
  59.2 0.9 reshape_squeeze_stack_squeeze.6
  60.1 1.0 copy.41
  61.2 1.0 reshape_squeeze_stack_squeeze.7
  62.9 0.7 copy.43
  63.6 0.7 pad_maximum_fusion
  65.5 1.2 convolution_add_fusion.1
  66.7 120.0 %while.20 = (s32[]{:T(128)}, f32[4,8,128]{2,1,0:T(8,128)S(1)}, f32[4,8,128]{2,1,0:T(8,128)S(1)}, f32[4,8,128,128]{3,2,1,0:T(8,128)S(1)}, bf16[2,128,512]{1,2,0:T...) while((s32[]{:T(128)}, f32[4,8,128]{2,1,0:T(8,128)S(1)}, ...), condition=%wide.region_7.8_spmd.clone, body=%wide.region_2.7_spmd.clone.sunk | while | flops 276324608 | bytes 14224691 | solution.py:439
  66.7 1.9 collective-permute-start
  68.6 14.9 %collective-permute-done = bf16[2,128,512]{1,2,0:T(8,128)(2,1)S(1)} collective-permute-done((bf16[2,128,512]{1,2,0:T(8,128)(2,1)}, bf16[2,128,512]{1,2,0:T(8,128)(2,1)S(1)}, u32[]{:S(2)}, u32[]{:S(2)}) %collective-permute-start) | collective-permute-done | bytes 262176 | tf_op jit(solution)/shard_map/while/body/eval_jaxpr/ppermute | solution.py:370
  83.5 2.7 conditional.3
  84.8 1.4 multiply_add_fusion
  86.2 0.7 copy.86
  86.9 1.9 collective-permute-start
  88.8 10.4 %collective-permute-done = bf16[2,128,512]{1,2,0:T(8,128)(2,1)S(1)} collective-permute-done((bf16[2,128,512]{1,2,0:T(8,128)(2,1)}, bf16[2,128,512]{1,2,0:T(8,128)(2,1)S(1)}, u32[]{:S(2)}, u32[]{:S(2)}) %collective-permute-start) | collective-permute-done | bytes 262176 | tf_op jit(solution)/shard_map/while/body/eval_jaxpr/ppermute | solution.py:370
  99.3 2.7 conditional.3
  100.5 1.4 multiply_add_fusion
  102.0 0.7 copy.86
  102.7 1.9 collective-permute-start
  104.6 16.3 %collective-permute-done = bf16[2,128,512]{1,2,0:T(8,128)(2,1)S(1)} collective-permute-done((bf16[2,128,512]{1,2,0:T(8,128)(2,1)}, bf16[2,128,512]{1,2,0:T(8,128)(2,1)S(1)}, u32[]{:S(2)}, u32[]{:S(2)}) %collective-permute-start) | collective-permute-done | bytes 262176 | tf_op jit(solution)/shard_map/while/body/eval_jaxpr/ppermute | solution.py:370
  120.9 2.7 conditional.3
  122.2 1.4 multiply_add_fusion
  123.6 0.7 copy.86
  124.3 1.9 collective-permute-start
  126.3 16.1 %collective-permute-done = bf16[2,128,512]{1,2,0:T(8,128)(2,1)S(1)} collective-permute-done((bf16[2,128,512]{1,2,0:T(8,128)(2,1)}, bf16[2,128,512]{1,2,0:T(8,128)(2,1)S(1)}, u32[]{:S(2)}, u32[]{:S(2)}) %collective-permute-start) | collective-permute-done | bytes 262176 | tf_op jit(solution)/shard_map/while/body/eval_jaxpr/ppermute | solution.py:370
  142.3 2.7 conditional.3
  143.6 1.4 multiply_add_fusion
  145.0 0.7 copy.86
  145.7 1.9 collective-permute-start
  147.7 15.8 %collective-permute-done = bf16[2,128,512]{1,2,0:T(8,128)(2,1)S(1)} collective-permute-done((bf16[2,128,512]{1,2,0:T(8,128)(2,1)}, bf16[2,128,512]{1,2,0:T(8,128)(2,1)S(1)}, u32[]{:S(2)}, u32[]{:S(2)}) %collective-permute-start) | collective-permute-done | bytes 262176 | tf_op jit(solution)/shard_map/while/body/eval_jaxpr/ppermute | solution.py:370
  163.4 0.7 copy.86
  164.1 1.9 collective-permute-start
  166.1 8.6 %collective-permute-done = bf16[2,128,512]{1,2,0:T(8,128)(2,1)S(1)} collective-permute-done((bf16[2,128,512]{1,2,0:T(8,128)(2,1)}, bf16[2,128,512]{1,2,0:T(8,128)(2,1)S(1)}, u32[]{:S(2)}, u32[]{:S(2)}) %collective-permute-start) | collective-permute-done | bytes 262176 | tf_op jit(solution)/shard_map/while/body/eval_jaxpr/ppermute | solution.py:370
  174.7 0.7 copy.86
  175.4 1.9 collective-permute-start
  177.3 8.6 %collective-permute-done = bf16[2,128,512]{1,2,0:T(8,128)(2,1)S(1)} collective-permute-done((bf16[2,128,512]{1,2,0:T(8,128)(2,1)}, bf16[2,128,512]{1,2,0:T(8,128)(2,1)S(1)}, u32[]{:S(2)}, u32[]{:S(2)}) %collective-permute-start) | collective-permute-done | bytes 262176 | tf_op jit(solution)/shard_map/while/body/eval_jaxpr/ppermute | solution.py:370
  186.0 0.7 copy.86
  186.7 1.9 copy.44
  188.6 1.9 divide_convert_fusion
  190.5 8.2 %fusion.18 = (f32[128]{0:T(128)S(1)}, bf16[128,2048]{1,0:T(8,128)(2,1)S(1)}) fusion(bf16[128,4096]{0,1:T(8,128)(2,1)S(1)} %bitcast.59, bf16[4096,2048]{1,0:T(8,128)(2,1)} %all-gather.5.cloned.1.call-done, bf16[1,128,2048]{2,1,0:T(8,128)(2,1)S(1)} %copy-done.2), kind=kOutput, calls=%fused_computation.31 | convolution fusion | flops 2149056512 | bytes 18874880 | tf_op jit(solution)/shard_map/dot_general | solution.py:448
  198.8 1.0 fusion.20.normed_ref
  200.4 95.5 %shard_map.122 = bf16[128,2048]{1,0:T(8,128)(2,1)} custom-call(bf16[128,2048]{1,0:T(8,128)(2,1)} %fusion.20.normed_ref, bf16[128,2048]{1,0:T(8,128)(2,1)} %copy-done, f32[16,8,128]{2,1,0:T(8,128)} %copy-done.4, bf16[2,2048,768]{2,1,0:T(8,128)(2,1)} %gate_hbm.1, bf16[2,2048,768]{2,1,0:T(8,128)(2,1)} %up_hbm.1, bf16[2,768,2048]{2,1,0:T(8,128)(2,1)} %down_hbm.1), custom_call_target="tpu_custom_call" | custom-call | tf_op jit(solution)/shard_map/pallas_call | solution.py:332
  295.9 1.9 copy.88
  (69 shorter events, 8.1 us)
Async XLA Ops:
  7.2 55.0 %copy-start.3 = (bf16[1,128,512]{2,1,0:T(8,128)(2,1)S(1)}, bf16[1,128,512]{2,1,0:T(8,128)(2,1)}, u32[]{:S(2)}) copy-start(bf16[1,128,512]{2,1,0:T(8,128)(2,1)} %param.17) | copy-start | bytes 393220
  7.2 55.1 %copy-start.1 = (bf16[1,128,4096]{2,1,0:T(8,128)(2,1)S(1)}, bf16[1,128,4096]{2,1,0:T(8,128)(2,1)}, u32[]{:S(2)}) copy-start(bf16[1,128,4096]{2,1,0:T(8,128)(2,1)} %param.15) | copy-start | bytes 3145732
  7.2 42.9 %all-gather.3.cloned.1.call-start = ((), (), s32[]{:S(2)}) async-start(), calls=%async_computation.1 | async-start | bytes 1179648 | tf_op jit(solution)/shard_map/all_gather | solution.py:447
  7.9 182.6 %all-gather.5.cloned.1.call-start = ((), (), s32[]{:S(2)}) async-start(), calls=%async_computation.2 | async-start | bytes 17825792 | tf_op jit(solution)/shard_map/all_gather | solution.py:450
  52.8 146.9 %all-to-all-start = ((f32[16,8,128]{2,1,0:T(8,128)}), f32[16,8,128]{2,1,0:T(8,128)S(1)}, u32[]{:S(2)}, u32[]{:S(2)}) async-start(f32[16,8,128]{2,1,0:T(8,128)} %pad.4), calls=%async_computation | async-start | bytes 131072 | tf_op jit(solution)/shard_map/all_to_all | solution.py:462
  66.7 16.8 %collective-permute-start = (bf16[2,128,512]{1,2,0:T(8,128)(2,1)}, bf16[2,128,512]{1,2,0:T(8,128)(2,1)S(1)}, u32[]{:S(2)}, u32[]{:S(2)}) collective-permute-start(bf16[2,128,512]{1,2,0:T(8,128)(2,1)} %get-tuple-element.326), channel_id=1, source_target_pairs={{0,16},{16,32},{32,48},{48,64},{64,80},{80,96},{96,112},{1,17},{17... | collective-permute-start | bytes 786440 | tf_op jit(solution)/shard_map/while/body/eval_jaxpr/ppermute | solution.py:370
  86.9 12.3 %collective-permute-start = (bf16[2,128,512]{1,2,0:T(8,128)(2,1)}, bf16[2,128,512]{1,2,0:T(8,128)(2,1)S(1)}, u32[]{:S(2)}, u32[]{:S(2)}) collective-permute-start(bf16[2,128,512]{1,2,0:T(8,128)(2,1)} %get-tuple-element.326), channel_id=1, source_target_pairs={{0,16},{16,32},{32,48},{48,64},{64,80},{80,96},{96,112},{1,17},{17... | collective-permute-start | bytes 786440 | tf_op jit(solution)/shard_map/while/body/eval_jaxpr/ppermute | solution.py:370
  102.7 18.3 %collective-permute-start = (bf16[2,128,512]{1,2,0:T(8,128)(2,1)}, bf16[2,128,512]{1,2,0:T(8,128)(2,1)S(1)}, u32[]{:S(2)}, u32[]{:S(2)}) collective-permute-start(bf16[2,128,512]{1,2,0:T(8,128)(2,1)} %get-tuple-element.326), channel_id=1, source_target_pairs={{0,16},{16,32},{32,48},{48,64},{64,80},{80,96},{96,112},{1,17},{17... | collective-permute-start | bytes 786440 | tf_op jit(solution)/shard_map/while/body/eval_jaxpr/ppermute | solution.py:370
  124.3 18.0 %collective-permute-start = (bf16[2,128,512]{1,2,0:T(8,128)(2,1)}, bf16[2,128,512]{1,2,0:T(8,128)(2,1)S(1)}, u32[]{:S(2)}, u32[]{:S(2)}) collective-permute-start(bf16[2,128,512]{1,2,0:T(8,128)(2,1)} %get-tuple-element.326), channel_id=1, source_target_pairs={{0,16},{16,32},{32,48},{48,64},{64,80},{80,96},{96,112},{1,17},{17... | collective-permute-start | bytes 786440 | tf_op jit(solution)/shard_map/while/body/eval_jaxpr/ppermute | solution.py:370
  145.7 17.7 %collective-permute-start = (bf16[2,128,512]{1,2,0:T(8,128)(2,1)}, bf16[2,128,512]{1,2,0:T(8,128)(2,1)S(1)}, u32[]{:S(2)}, u32[]{:S(2)}) collective-permute-start(bf16[2,128,512]{1,2,0:T(8,128)(2,1)} %get-tuple-element.326), channel_id=1, source_target_pairs={{0,16},{16,32},{32,48},{48,64},{64,80},{80,96},{96,112},{1,17},{17... | collective-permute-start | bytes 786440 | tf_op jit(solution)/shard_map/while/body/eval_jaxpr/ppermute | solution.py:370
  164.1 10.6 %collective-permute-start = (bf16[2,128,512]{1,2,0:T(8,128)(2,1)}, bf16[2,128,512]{1,2,0:T(8,128)(2,1)S(1)}, u32[]{:S(2)}, u32[]{:S(2)}) collective-permute-start(bf16[2,128,512]{1,2,0:T(8,128)(2,1)} %get-tuple-element.326), channel_id=1, source_target_pairs={{0,16},{16,32},{32,48},{48,64},{64,80},{80,96},{96,112},{1,17},{17... | collective-permute-start | bytes 786440 | tf_op jit(solution)/shard_map/while/body/eval_jaxpr/ppermute | solution.py:370
  175.4 10.6 %collective-permute-start = (bf16[2,128,512]{1,2,0:T(8,128)(2,1)}, bf16[2,128,512]{1,2,0:T(8,128)(2,1)S(1)}, u32[]{:S(2)}, u32[]{:S(2)}) collective-permute-start(bf16[2,128,512]{1,2,0:T(8,128)(2,1)} %get-tuple-element.326), channel_id=1, source_target_pairs={{0,16},{16,32},{32,48},{48,64},{64,80},{80,96},{96,112},{1,17},{17... | collective-permute-start | bytes 786440 | tf_op jit(solution)/shard_map/while/body/eval_jaxpr/ppermute | solution.py:370
  188.6 1.9 copy-start.2
  190.5 8.3 %copy-start.5 = (f32[2048]{0:T(1024)S(1)}, f32[2048]{0:T(1024)}, u32[]{:S(2)}) copy-start(f32[2048]{0:T(1024)} %param.20) | copy-start | bytes 24580
  198.8 1.0 copy-start
  199.8 0.6 copy-start.4
Sparse Core Ops, SparseCore 0:
  9.7 40.3 all-gather.2
  52.4 120.3 all-gather.4

commit v2 on v1

--- a/solution.py
+++ b/solution.py
@@ -140,20 +140,23 @@
     def part_copy(chip):
         return send(parts.at[chip * 2 + other], sib_parts.at[chip], part, chip, sibling)
 
+    first_row = lax.rem(me, 4) * 2
+
     def selection(block):
-        both = share_ref[block]
-        chosen = both > 0.0
+        share_rows = jnp.concatenate(
+            [
+                jnp.broadcast_to(share_ref[block, pl.ds(first_row + j, 1)], (CAP, TOK))
+                for j in range(2)
+            ],
+            axis=0,
+        )
+        chosen = share_rows > 0.0
         count = jnp.dot(
-            chosen.astype(jnp.bfloat16), up_to, preferred_element_type=jnp.float32
+            chosen.astype(jnp.float32).astype(jnp.bfloat16),
+            up_to,
+            preferred_element_type=jnp.float32,
         )
-        place = jnp.where(chosen, count - 1.0, -1.0)
-        place_rows = jnp.concatenate(
-            [jnp.broadcast_to(place[j : j + 1], (CAP, TOK)) for j in range(2)], axis=0
-        )
-        share_rows = jnp.concatenate(
-            [jnp.broadcast_to(both[j : j + 1], (CAP, TOK)) for j in range(2)], axis=0
-        )
-        picked = place_rows == slot_of_row
+        picked = chosen & (count - 1.0 == slot_of_row)
         slot_share = jnp.sum(jnp.where(picked, share_rows, 0.0), axis=1, keepdims=True)
         return picked.astype(jnp.float32), slot_share
 
@@ -370,26 +373,355 @@
     return lax.ppermute(shard, axis, pairs)
 
 
-def attend_block(state_now, key_value_portion, begin_row, query_head_rows, query_place):
-    row_top, row_total, accum = state_now
-    key_total = key_value_portion.shape[1]
-    key_head_rows = key_value_portion[0].reshape(key_total, KEY_VALUE_HEADS, HEAD_SIZE)
-    value_head_rows = key_value_portion[1].reshape(key_total, KEY_VALUE_HEADS, HEAD_SIZE)
-    raw_scores = jnp.einsum(
-        "tngd,und->ngtu", query_head_rows, key_head_rows, preferred_element_type=jnp.float32
-    ) * HEAD_SIZE ** (-0.5)
-    key_place = begin_row + jnp.arange(key_total, dtype=jnp.int32)
-    allowed = query_place[:, None] >= key_place[None, :]
-    raw_scores = jnp.where(allowed, raw_scores, mask_fill_value)
-    new_top = jnp.maximum(row_top, jnp.max(raw_scores, axis=-1))
-    factor = jnp.exp(row_top - new_top)
-    exp_scores = jnp.where(allowed, jnp.exp(raw_scores - new_top[..., None]), 0.0)
-    row_total = row_total * factor + jnp.sum(exp_scores, axis=-1)
-    weights = exp_scores.astype(jnp.bfloat16)
-    accum = accum * factor[..., None] + jnp.einsum(
-        "ngtu,und->ngtd", weights, value_head_rows, preferred_element_type=jnp.float32
+PIECES = ((0, 224, "xyz"), (224, 160, "yzx"), (384, 128, "zxy"))
+
+
+def front_kernel(
+    queries_ref,
+    keys_ref,
+    values_ref,
+    resid_ref,
+    weight_ref,
+    gain_ref,
+    ids_ref,
+    gates_ref,
+    normed_ref,
+    attn_resid_ref,
+    shares_ref,
+    weight,
+    kv,
+    stacked,
+    attended,
+    to_sibling,
+    from_sibling,
+    share_tiles,
+    shares_in,
+    kv_send,
+    kv_recv,
+    w_send,
+    w_recv,
+    share_send,
+    share_recv,
+    att_send,
+    att_recv,
+    proj_send,
+    proj_recv,
+):
+    ctx, exp = lax.axis_index("ctx"), lax.axis_index("exp")
+    x_low, y = ctx // 4, lax.rem(ctx, 4)
+    z, x_high, core = exp // 4, lax.rem(exp // 2, 2), lax.rem(exp, 2)
+    here = {"x": x_high * 2 + x_low, "y": y, "z": z}
+    other = 1 - core
+    sibling = {"ctx": ctx, "exp": exp + 1 - 2 * core}
+
+    def device(x, y_at, z_at):
+        return {"ctx": lax.rem(x, 2) * 4 + y_at, "exp": z_at * 4 + (x // 2) * 2 + core}
+
+    def neighbour(axis, by):
+        there = dict(here)
+        there[axis] = lax.rem(here[axis] + by, 4)
+        return device(there["x"], there["y"], there["z"])
+
+    partner = {"ctx": (1 - x_low) * 4 + y, "exp": exp}
+
+    def send(src, dst, sems, number, peer):
+        return pltpu.make_async_remote_copy(
+            src_ref=src,
+            dst_ref=dst,
+            send_sem=sems[0].at[number],
+            recv_sem=sems[1].at[number],
+            device_id=peer,
+            device_id_type=MESH,
+        )
+
+    kv[ctx, 0] = keys_ref[...]
+    kv[ctx, 1] = values_ref[...]
+    weight[x_high, x_low, y, :, pl.ds(pl.multiple_of(z * 128, 128), 128)] = weight_ref[...]
+
+    barrier = pltpu.get_barrier_semaphore()
+    for step in range(1, 16):
+        pl.semaphore_signal(
+            barrier,
+            inc=1,
+            device_id={"ctx": ctx, "exp": lax.rem(exp + step, 16)},
+            device_id_type=MESH,
+        )
+    for axis in ("x", "y"):
+        for by in (1, 3):
+            pl.semaphore_signal(
+                barrier, inc=1, device_id=neighbour(axis, by), device_id_type=MESH
+            )
+    pl.semaphore_wait(barrier, 19)
+
+    kv_sems = (kv_send, kv_recv)
+
+    def kv_block(dy, dx):
+        return lax.rem(x_low + dx, 2) * 4 + lax.rem(y + dy, 4)
+
+    y_up, y_down = neighbour("y", 1), neighbour("y", 3)
+
+    def kv_copy(number, block, part, peer):
+        ref = kv.at[block] if part is None else kv.at[block, part]
+        return send(ref, ref, kv_sems, number, peer)
+
+    kv_out = (
+        kv_copy(0, kv_block(0, 0), None, y_up),
+        kv_copy(1, kv_block(0, 0), None, y_down),
+        kv_copy(2, kv_block(0, 0), None, partner),
+        kv_copy(3, kv_block(3, 0), 0, y_up),
+        kv_copy(4, kv_block(1, 0), 1, y_down),
+        kv_copy(5, kv_block(0, 1), None, y_up),
+        kv_copy(6, kv_block(0, 1), None, y_down),
+        kv_copy(7, kv_block(2, 0), None, partner),
     )
-    return (new_top, row_total, accum)
+    kv_in = (
+        kv_copy(0, kv_block(3, 0), None, y_up),
+        kv_copy(1, kv_block(1, 0), None, y_down),
+        kv_copy(2, kv_block(0, 1), None, partner),
+        kv_copy(3, kv_block(2, 0), 0, y_up),
+        kv_copy(4, kv_block(2, 0), 1, y_down),
+        kv_copy(5, kv_block(3, 1), None, y_up),
+        kv_copy(6, kv_block(1, 1), None, y_down),
+        kv_copy(7, kv_block(2, 1), None, partner),
+    )
+
+    w_sems = (w_send, w_recv)
+
+    def segment(piece, stage, by, rows):
+        order = PIECES[piece][2]
+        at = {}
+        for axis in order[stage:]:
+            at[axis] = here[axis]
+        at[order[stage]] = lax.rem(here[order[stage]] + by, 4)
+        full = slice(None)
+        lanes = pl.ds(pl.multiple_of(at["z"] * 128, 128), 128) if "z" in at else full
+        x_pair = (at["x"] // 2, lax.rem(at["x"], 2)) if "x" in at else (full, full)
+        return weight.at[x_pair[0], x_pair[1], at.get("y", full), rows, lanes]
+
+    def w_copies(piece, stage):
+        first, height, order = PIECES[piece]
+        whole = pl.ds(first, height)
+        halves = (pl.ds(first, height // 2), pl.ds(first + height // 2, height // 2))
+        axis = order[stage]
+        up, down = neighbour(axis, 1), neighbour(axis, 3)
+        base = (piece * 3 + stage) * 4
+        out, arrive = [], []
+        for number, (sent, got, rows, peer) in enumerate(
+            (
+                (0, 3, whole, up),
+                (0, 1, whole, down),
+                (3, 2, halves[0], up),
+                (1, 2, halves[1], down),
+            )
+        ):
+            mine = segment(piece, stage, sent, rows)
+            theirs = segment(piece, stage, got, rows)
+            out.append(send(mine, mine, w_sems, base + number, peer))
+            arrive.append(send(theirs, theirs, w_sems, base + number, peer))
+        return out, arrive
+
+    w_plan = [[w_copies(piece, stage) for stage in range(3)] for piece in range(3)]
+
+    def w_begin(stage):
+        for piece in range(3):
+            for number in (0, 1):
+                w_plan[piece][stage][0][number].start()
+
+    def w_forward(stage):
+        for piece in range(3):
+            out, arrive = w_plan[piece][stage]
+            for number in (0, 1):
+                arrive[number].wait_recv()
+                out[number + 2].start()
+
+    def w_end(stage):
+        for piece in range(3):
+            for number in (2, 3):
+                w_plan[piece][stage][1][number].wait_recv()
+
+    for number in (0, 1, 2):
+        kv_out[number].start()
+    w_begin(0)
+
+    gates = gates_ref[...]
+    shares = gates / jnp.sum(gates, axis=1, keepdims=True)
+    ids = ids_ref[...]
+    lane = lax.broadcasted_iota(jnp.int32, (TOK, TOK), 1)
+    dense = jnp.zeros((TOK, TOK), jnp.float32)
+    for k in range(TOPK):
+        dense = dense + jnp.where(ids[:, k : k + 1] == lane, shares[:, k : k + 1], 0.0)
+    flipped = dense.T
+    for group in range(4):
+        share_tiles[group] = flipped[group * 8 : (group + 1) * 8]
+    shares_in[exp] = share_tiles[exp // 4]
+    share_sems = (share_send, share_recv)
+    share_out, share_arrive = [], []
+    for step in range(1, 16):
+        there = lax.rem(exp + step, 16)
+        share_out.append(
+            send(
+                share_tiles.at[there // 4],
+                shares_in.at[exp],
+                share_sems,
+                step,
+                {"ctx": ctx, "exp": there},
+            )
+        )
+        behind = lax.rem(exp + 16 - step, 16)
+        share_arrive.append(
+            send(
+                share_tiles.at[there // 4],
+                shares_in.at[behind],
+                share_sems,
+                step,
+                {"ctx": ctx, "exp": there},
+            )
+        )
+        share_out[-1].start()
+
+    w_forward(0)
+    for head in range(QUERY_HEAD_COUNT):
+        stacked[head // 4, (head % 4) * TOK : (head % 4 + 1) * TOK] = queries_ref[
+            :, head * HEAD_SIZE : (head + 1) * HEAD_SIZE
+        ]
+    w_end(0)
+    w_begin(1)
+    for number in (0, 1, 2):
+        kv_in[number].wait_recv()
+    for number in (3, 4, 5, 6):
+        kv_out[number].start()
+    w_forward(1)
+    kv_in[3].wait_recv()
+    kv_in[4].wait_recv()
+    kv_out[7].start()
+    w_end(1)
+    w_begin(2)
+    for number in (5, 6, 7):
+        kv_in[number].wait_recv()
+
+    att_sems = (att_send, att_recv)
+
+    def att_copy(number):
+        part = attended.at[core, :, pl.ds(pl.multiple_of(number * 512, 512), 512)]
+        return send(part, part, att_sems, number, sibling)
+
+    keys_total = 8 * TOK
+    scale = HEAD_SIZE**-0.5 * 1.4426950408889634
+
+    def heads(quad, carry):
+        lanes = pl.ds(pl.multiple_of((quad // 2) * HEAD_SIZE, HEAD_SIZE), HEAD_SIZE)
+        keys_here = jnp.concatenate([kv[block, 0, :, lanes] for block in range(8)], axis=0)
+        values_here = jnp.concatenate([kv[block, 1, :, lanes] for block in range(8)], axis=0)
+        values_wide = jnp.concatenate([values_here, jnp.ones_like(values_here)], axis=1)
+        for part in range(4):
+            scores = lax.dot_general(
+                stacked[quad, part * TOK : (part + 1) * TOK],
+                keys_here,
+                (((1,), (1,)), ((), ())),
+                preferred_element_type=jnp.float32,
+            )
+            query_at = lax.broadcasted_iota(jnp.int32, (TOK, keys_total), 0) + ctx * TOK
+            key_at = lax.broadcasted_iota(jnp.int32, (TOK, keys_total), 1)
+            scores = jnp.where(query_at >= key_at, scores, mask_fill_value)
+            top = jnp.max(scores, axis=1, keepdims=True)
+            weights = jnp.exp2((scores - top) * scale).astype(jnp.bfloat16)
+            result = jnp.dot(weights, values_wide, preferred_element_type=jnp.float32)
+            attended[
+                core,
+                :,
+                pl.ds(pl.multiple_of(quad * 512 + part * HEAD_SIZE, HEAD_SIZE), HEAD_SIZE),
+            ] = (result[:, :HEAD_SIZE] / result[:, HEAD_SIZE:]).astype(jnp.bfloat16)
+        att_copy(quad).start()
+        return carry
+
+    lax.fori_loop(0, 8, heads, 0)
+    w_forward(2)
+    for number in range(8):
+        part = attended.at[other, :, pl.ds(number * 512, 512)]
+        send(part, part, att_sems, number, sibling).wait_recv()
+    w_end(2)
+
+    def project(half, carry):
+        rows = weight[half].reshape(8 * 512, 512)
+        mine = jnp.dot(attended[core], rows, preferred_element_type=jnp.float32)
+        theirs = jnp.dot(attended[other], rows, preferred_element_type=jnp.float32)
+        to_sibling[half] = theirs
+        from_sibling[2 + half] = mine
+        return carry
+
+    lax.fori_loop(0, 2, project, 0)
+    swap = send(to_sibling, from_sibling.at[pl.ds(0, 2)], (proj_send, proj_recv), 0, sibling)
+    swap.start()
+
+    def place(first, which):
+        for half in range(2):
+            for depth in range(4):
+                lanes = pl.ds(
+                    pl.multiple_of(depth * 512 + half * 256 + which * 128, 128), 128
+                )
+                attn_resid_ref[:, lanes] = (
+                    resid_ref[:, lanes].astype(jnp.float32)
+                    + from_sibling[first + half, :, depth * 128 : (depth + 1) * 128]
+                ).astype(jnp.bfloat16)
+
+    place(2, core)
+    for arriving in share_arrive:
+        arriving.wait_recv()
+    shares_ref[...] = shares_in[...]
+    swap.wait_recv()
+    place(0, other)
+    wide = attn_resid_ref[...].astype(jnp.float32)
+    scale_row = lax.rsqrt(jnp.mean(wide * wide, axis=1, keepdims=True) + norm_eps)
+    normed_ref[...] = (wide * scale_row * gain_ref[...]).astype(jnp.bfloat16)
+
+    for copy in (*kv_out, *share_out):
+        copy.wait_send()
+    for piece in range(3):
+        for stage in range(3):
+            for copy in w_plan[piece][stage][0]:
+                copy.wait_send()
+    for number in range(8):
+        att_copy(number).wait_send()
+    swap.wait_send()
+
+
+def front(queries, keys, values, resid, out_weight, norm_gain, route_ids, route_gates):
+    vmem = pl.BlockSpec(memory_space=pltpu.VMEM)
+    dma = pltpu.SemaphoreType.DMA
+    bf16, f32 = jnp.bfloat16, jnp.float32
+    return pl.pallas_call(
+        front_kernel,
+        out_shape=(
+            jax.ShapeDtypeStruct((TOK, D), bf16),
+            jax.ShapeDtypeStruct((TOK, D), bf16),
+            jax.ShapeDtypeStruct((16, 8, TOK), f32),
+        ),
+        in_specs=[vmem] * 8,
+        out_specs=(vmem, vmem, vmem),
+        scratch_shapes=[
+            pltpu.VMEM((2, 2, 4, 512, 512), bf16),
+            pltpu.VMEM((8, 2, TOK, 512), bf16),
+            pltpu.VMEM((8, 512, HEAD_SIZE), bf16),
+            pltpu.VMEM((2, TOK, 4096), bf16),
+            pltpu.VMEM((2, TOK, 512), f32),
+            pltpu.VMEM((4, TOK, 512), f32),
+            pltpu.VMEM((4, 8, TOK), f32),
+            pltpu.VMEM((16, 8, TOK), f32),
+            dma((8,)),
+            dma((8,)),
+            dma((36,)),
+            dma((36,)),
+            dma((16,)),
+            dma((16,)),
+            dma((8,)),
+            dma((8,)),
+            dma((1,)),
+            dma((1,)),
+        ],
+        compiler_params=pltpu.CompilerParams(
+            collective_id=0, has_side_effects=True, vmem_limit_bytes=40 << 20
+        ),
+    )(queries, keys, values, resid, out_weight, norm_gain, route_ids, route_gates)
 
 
 def local(
@@ -405,62 +737,17 @@
     route_ids,
     route_gates,
 ):
-    token_rows = queries.shape[1]
-    ctx_count = lax.axis_size("ctx")
-    exp_count = lax.axis_size("exp")
-    my_block = lax.axis_index("ctx")
-    query_group = QUERY_HEAD_COUNT // KEY_VALUE_HEADS
-    query_head_rows = queries[0].reshape(token_rows, KEY_VALUE_HEADS, query_group, HEAD_SIZE)
-    query_place = my_block * token_rows + jnp.arange(token_rows, dtype=jnp.int32)
-    kv_local = jnp.stack([keys[0], values[0]])
-    state_first = (
-        jnp.full((KEY_VALUE_HEADS, query_group, token_rows), mask_fill_value, jnp.float32),
-        jnp.zeros((KEY_VALUE_HEADS, query_group, token_rows), jnp.float32),
-        jnp.zeros((KEY_VALUE_HEADS, query_group, token_rows, HEAD_SIZE), jnp.float32),
+    normed, attn_resid, shares = front(
+        queries[0],
+        keys[0],
+        values[0],
+        resid[0],
+        out_weight,
+        norm_gain[None],
+        route_ids[0],
+        route_gates[0],
     )
-    state_now = attend_block(
-        state_first, kv_local, my_block * token_rows, query_head_rows, query_place
-    )
-
-    def circle_step(step_num, carried):
-        state_in, key_value_portion = carried
-        key_value_portion = from_behind(key_value_portion, "ctx", 1)
-        source = my_block - step_num
-        state_out = lax.cond(
-            source >= 0,
-            lambda held: attend_block(
-                held, key_value_portion, source * token_rows, query_head_rows, query_place
-            ),
-            lambda held: held,
-            state_in,
-        )
-        return (state_out, key_value_portion)
-
-    state_now, kv_last = lax.fori_loop(1, ctx_count, circle_step, (state_now, kv_local))
-    row_top, row_total, accum = state_now
-    attention = (
-        (accum / row_total[..., None])
-        .transpose(2, 0, 1, 3)
-        .reshape(token_rows, QUERY_HEAD_COUNT * HEAD_SIZE)
-        .astype(jnp.bfloat16)
-    )
-    all_rows = lax.all_gather(out_weight, "ctx", axis=0, tiled=True)
-    projected = jnp.dot(
-        attention,
-        lax.all_gather(all_rows, "exp", axis=1, tiled=True),
-        preferred_element_type=jnp.float32,
-    )
-    attn_resid = (resid[0].astype(jnp.float32) + projected).astype(jnp.bfloat16)
-    resid_wide = attn_resid.astype(jnp.float32)
-    scale_row = lax.rsqrt(jnp.mean(resid_wide * resid_wide, axis=-1, keepdims=True) + norm_eps)
-    normed = (resid_wide * scale_row * norm_gain).astype(jnp.bfloat16)
-    gate_rows = route_gates[0]
-    shares = gate_rows / jnp.sum(gate_rows, axis=-1, keepdims=True)
-    hits = route_ids[0][:, :, None] == jnp.arange(EXPERTS, dtype=jnp.int32)[None, None, :]
-    dense = jnp.sum(jnp.where(hits, shares[:, :, None], 0.0), axis=1)
-    wanted = jnp.pad(dense.T.reshape(exp_count, 2, token_rows), ((0, 0), (0, 6), (0, 0)))
-    shares_here = lax.all_to_all(wanted, "exp", split_axis=0, concat_axis=0, tiled=True)
-    layer_out = moe(normed, attn_resid, shares_here, expert_gate, expert_up, expert_down)
+    layer_out = moe(normed, attn_resid, shares, expert_gate, expert_up, expert_down)
     return (attn_resid[None], layer_out[None])
 
 

time: 307 us -> 185 us (0.60)
  waiting for transfers between devices: 134 us -> 0 us
  Pallas kernels: 95.5 us -> 171 us
  starting transfers between devices: 19.8 us -> 0 us
  matrix products: 17.7 us -> 0 us
  between operations: 14.2 us -> 0.68 us
  other arithmetic: 9.04 us -> 0 us
    ppermute x7 -> x0, waiting for transfers between devices: 90.8 us -> none  [from_behind(): return lax.ppermute(shard, axis, pairs)]
    pallas_call x0 -> x1, Pallas kernels: none -> 72.2 us  [front(): pl.pallas_call(front_kernel, out_shape=(jax.ShapeDtypeStruct((TOK, D), bf...]
    all_gather x2 -> x0, waiting for transfers between devices: 42.1 us -> none  [the longest x1 42.1 us: local(): all_rows = lax.all_gather(out_weight, 'ctx', axis=0, tiled=True)]
    dot_general x11 -> x0, matrix products: 17.7 us -> none  [the longest x1 8.23 us: local(): jnp.dot(attention, lax.all_gather(all_rows, 'exp', axis=1, tiled=True), p...]
    ppermute x7 -> x0, starting transfers between devices: 13.4 us -> none  [from_behind(): return lax.ppermute(shard, axis, pairs)]
    unnamed x17 -> x24, local copies, waits for them, and re-layouts: 4.99 us -> 12.1 us
    while x8 -> x0, local copies, waits for them, and re-layouts: 6.79 us -> none
    all_to_all x1 -> x0, starting transfers between devices: 6.34 us -> none  [local(): lax.all_to_all(wanted, 'exp', split_axis=0, concat_axis=0, tiled=True)]
  transfers between devices with their start and end apart: 10 -> 0, of which waited for: 8 -> 0; matrix products, arithmetic and copies ran while one was open for 13% -> 0% of each run, Pallas kernels for 0% -> 0%
where the time goes in v2:
time: 185 us; the launch traced here: 184 us
  Pallas kernels  171 us (92%)
  local copies, waits for them, and re-layouts  12.1 us (7%)
    pallas_call x1, Pallas kernels, moe(): pl.pallas_call(moe_kernel, out_shape=jax.ShapeDtypeStruct((TOK, D), bf16)...  98.7 us
    pallas_call x1, Pallas kernels, front(): pl.pallas_call(front_kernel, out_shape=(jax.ShapeDtypeStruct((TOK, D), bf...  72.2 us
    unnamed x24, local copies, waits for them, and re-layouts  12.1 us

profile of v2, /device:TPU:2, one launch (start us, length us, event | category | flops | bytes accessed | tf_op | source)
XLA Modules:
  0.0 183.6 jit_solution(14071512541371637775)
XLA Ops:
  0.6 0.8 copy.13
  1.4 0.8 copy.14
  2.2 0.0 copy-start.2
  2.2 1.2 copy-done.2
  3.4 0.0 copy-start.4
  3.4 1.0 copy-done.4
  4.5 0.0 copy-start.5
  4.5 0.9 copy-done.5
  5.4 0.0 copy-start.6
  5.4 0.9 copy-done.6
  6.3 0.0 copy-start.7
  6.3 0.9 copy-done.7
  7.2 0.0 copy-start.9
  7.2 0.7 copy-done.9
  7.9 72.2 %shard_map.122 = (bf16[128,2048]{1,0:T(8,128)(2,1)S(1)}, bf16[128,2048]{1,0:T(8,128)(2,1)S(1)}, f32[16,8,128]{2,1,0:T(8,128)S(1)}) custom-call(bf16[128,4096]{1,0:T(8,128)(2,1)S(1)} %bitcast.10, bf16[128,512]{1,0:T(8,128)(2,1)S(1)} %bitcast.14, bf16[128,512]{1,0:T(8,128)(2,1)S(1)} %bitcast.15, bf16[128,2048]{1,0:T(8,128)(2,1)S(1)} %bitcast.11, ...), custom_call_target="tpu_custom_call" | custom-call | tf_op jit(solution)/shard_map/pallas_call | solution.py:692
  80.1 0.0 copy-start
  80.1 0.8 copy-done
  80.9 0.0 copy-start.3
  80.9 0.8 copy-done.3
  81.7 0.0 copy-start.8
  81.7 0.6 copy-done.8
  82.3 0.0 copy-start.1
  82.3 98.7 %shard_map.123 = bf16[128,2048]{1,0:T(8,128)(2,1)} custom-call(bf16[128,2048]{1,0:T(8,128)(2,1)} %copy-done.3, bf16[128,2048]{1,0:T(8,128)(2,1)} %copy-done, f32[16,8,128]{2,1,0:T(8,128)} %copy-done.8, bf16[2,2048,768]{2,1,0:T(8,128)(2,1)} %gate_hbm.1, bf16[2,2048,768]{2,1,0:T(8,128)(2,1)} %up_hbm.1, bf16[2,768,2048]{2,1,0:T(8,128)(2,1)} %down_hbm.1), custom_call_target="tpu_custom_call" | custom-call | tf_op jit(solution)/shard_map/pallas_call | solution.py:335
  181.0 0.0 copy-done.1
  181.0 0.8 copy.17
  181.8 1.9 %copy.18 = bf16[1,128,2048]{2,1,0:T(8,128)(2,1)} copy(bf16[1,128,2048]{2,1,0:T(8,128)(2,1)} %bitcast.17) | data formatting | bytes 1048576
Async XLA Ops:
  2.2 1.2 copy-start.2
  3.4 1.0 copy-start.4
  4.5 0.9 copy-start.5
  5.4 0.9 copy-start.6
  6.3 0.9 copy-start.7
  7.2 0.7 copy-start.9
  80.1 0.8 copy-start
  80.9 0.8 copy-start.3
  81.7 0.6 copy-start.8
  82.3 98.7 %copy-start.1 = (bf16[128,2048]{1,0:T(8,128)(2,1)S(1)}, bf16[128,2048]{1,0:T(8,128)(2,1)}, u32[]{:S(2)}) copy-start(bf16[128,2048]{1,0:T(8,128)(2,1)} %copy-done) | copy-start | bytes 1572868

commit v3 on v1

v3 whole, which is shorter than its diff:
```python
import functools

import jax
import jax.numpy as jnp
from jax import lax
from jax.experimental import pallas as pl
from jax.experimental.pallas import tpu as pltpu
from jax.sharding import PartitionSpec as P

QUERY_HEAD_COUNT = 32
HEAD_SIZE = 128
TOPK = 8
CAP = 64
TOK = 128
D = 2048
FF = 768
EXPERTS = 32
MESH = pl.DeviceIdType.MESH

norm_eps = 1e-06
mask_fill_value = -1e30

RELATIONS = ((0, 0), (3, 0), (1, 0), (0, 1), (2, 0), (3, 1), (1, 1), (2, 1))
PAIRS = ((0, 3), (1, 2), (4, 7), (5, 6))
PIECES = ((0, 208, 112, "xyz"), (208, 160, 80, "yzx"), (368, 144, 80, "zxy"))


def layer_kernel(
    queries_hbm,
    keys_hbm,
    values_hbm,
    resid_hbm,
    weight_hbm,
    gain_hbm,
    ids_hbm,
    gates_hbm,
    gate_hbm,
    up_hbm,
    down_hbm,
    attn_resid_ref,
    out_ref,
    weight,
    kv,
    stacked,
    attended,
    to_sibling,
    from_sibling,
    resid,
    gain,
    ids,
    gates,
    share_tiles,
    shares_in,
    gate_w,
    up_w,
    down_w,
    blocks,
    sib_parts,
    half_in,
    full_in,
    far_in,
    hop_in,
    slots_in,
    slots_out,
    act,
    pick,
    scatter,
    load_sem,
    query_sem,
    expert_sem,
    kv_send,
    kv_recv,
    w_send,
    w_recv,
    share_send,
    share_recv,
    att_send,
    att_recv,
    proj_send,
    proj_recv,
    ag_send,
    ag_recv,
    sib_send,
    sib_recv,
    part_send,
    part_recv,
    rs_send,
    rs_recv,
):
    ctx, exp = lax.axis_index("ctx"), lax.axis_index("exp")
    x_low, y = ctx // 4, lax.rem(ctx, 4)
    z, x_high, core = exp // 4, lax.rem(exp // 2, 2), lax.rem(exp, 2)
    here = {"x": x_high * 2 + x_low, "y": y, "z": z}
    other = 1 - core

    def device(x, y_at, z_at):
        return {"ctx": lax.rem(x, 2) * 4 + y_at, "exp": z_at * 4 + (x // 2) * 2 + core}

    def neighbour(axis, by):
        there = dict(here)
        there[axis] = lax.rem(here[axis] + by, 4)
        return device(there["x"], there["y"], there["z"])

    sibling = {"ctx": ctx, "exp": exp + 1 - 2 * core}
    partner = {"ctx": (1 - x_low) * 4 + y, "exp": exp}
    y_up, y_down = neighbour("y", 1), neighbour("y", 3)
    z_up, z_down, x_over = neighbour("z", 1), neighbour("z", 3), neighbour("x", 2)

    def send(src, dst, sems, number, peer):
        return pltpu.make_async_remote_copy(
            src_ref=src,
            dst_ref=dst,
            send_sem=sems[0].at[number],
            recv_sem=sems[1].at[number],
            device_id=peer,
            device_id_type=MESH,
        )

    own_weight = weight.at[
        x_high, x_low, y, :, pl.ds(pl.multiple_of(z * 128, 128), 128)
    ]
    loads = []
    for number, (src, dst) in enumerate(
        (
            (weight_hbm, own_weight),
            (keys_hbm, kv.at[ctx, 0]),
            (values_hbm, kv.at[ctx, 1]),
            (ids_hbm, ids),
            (gates_hbm, gates),
            (gain_hbm, gain),
            (resid_hbm, resid),
        )
    ):
        loads.append(pltpu.make_async_copy(src, dst, load_sem.at[number]))
        loads[-1].start()
    query_loads = []
    for head in range(QUERY_HEAD_COUNT):
        query_loads.append(
            pltpu.make_async_copy(
                queries_hbm.at[:, pl.ds(head * HEAD_SIZE, HEAD_SIZE)],
                stacked.at[head // 4, pl.ds((head % 4) * TOK, TOK)],
                query_sem.at[head],
            )
        )
        query_loads[-1].start()

    barrier = pltpu.get_barrier_semaphore()
    for step in range(1, 16):
        pl.semaphore_signal(
            barrier,
            inc=1,
            device_id={"ctx": ctx, "exp": lax.rem(exp + step, 16)},
            device_id_type=MESH,
        )
    for by in (1, 2, 3):
        pl.semaphore_signal(barrier, inc=1, device_id=neighbour("y", by), device_id_type=MESH)
    for by in (1, 3):
        pl.semaphore_signal(barrier, inc=1, device_id=neighbour("x", by), device_id_type=MESH)
    pl.semaphore_wait(barrier, 20)

    w_sems = (w_send, w_recv)

    def segment(piece, stage, by, rows):
        order = PIECES[piece][3]
        at = {}
        for axis in order[stage:]:
            at[axis] = here[axis]
        at[order[stage]] = lax.rem(here[order[stage]] + by, 4)
        full = slice(None)
        lanes = pl.ds(pl.multiple_of(at["z"] * 128, 128), 128) if "z" in at else full
        x_pair = (at["x"] // 2, lax.rem(at["x"], 2)) if "x" in at else (full, full)
        return weight.at[x_pair[0], x_pair[1], at.get("y", full), rows, lanes]

    def w_copies(piece, stage):
        first, height, cut, order = PIECES[piece]
        axis = order[stage]
        whole = pl.ds(first, height)
        top, bottom = pl.ds(first, cut), pl.ds(first + cut, height - cut)
        if stage < 2:
            base = piece * 12 + stage * 3
            moves = [(0, 4 - by, whole, neighbour(axis, by)) for by in (1, 3, 2)]
        else:
            base = piece * 12 + 6
            up, down = neighbour(axis, 1), neighbour(axis, 3)
            moves = [
                (0, 3, top, up),
                (0, 1, bottom, down),
                (0, 3, bottom, up),
                (0, 1, top, down),
                (3, 2, top, up),
                (1, 2, bottom, down),
            ]
        out, arrive = [], []
        for number, (sent, got, rows, peer) in enumerate(moves):
            mine = segment(piece, stage, sent, rows)
            theirs = segment(piece, stage, got, rows)
            out.append(send(mine, mine, w_sems, base + number, peer))
            arrive.append(send(theirs, theirs, w_sems, base + number, peer))
        return out, arrive

    w_plan = [[w_copies(piece, stage) for stage in range(3)] for piece in range(3)]

    def w_begin(stage):
        for number in range(3 if stage < 2 else 4):
            for piece in range(3):
                w_plan[piece][stage][0][number].start()

    def w_end(stage):
        for piece in range(3):
            for number in (0, 1, 2) if stage < 2 else (2, 3, 4, 5):
                w_plan[piece][stage][1][number].wait_recv()

    def w_forward(piece):
        out, arrive = w_plan[piece][2]
        arrive[0].wait_recv()
        out[4].start()
        arrive[1].wait_recv()
        out[5].start()

    kv_sems = (kv_send, kv_recv)

    def kv_block(dy, dx):
        return lax.rem(x_low + dx, 2) * 4 + lax.rem(y + dy, 4)

    def kv_copy(number, block, part, peer):
        ref = kv.at[block] if part is None else kv.at[block, part]
        return send(ref, ref, kv_sems, number, peer)

    kv_out = (
        kv_copy(0, kv_block(0, 0), None, y_up),
        kv_copy(1, kv_block(0, 0), None, y_down),
        kv_copy(2, kv_block(0, 0), None, partner),
        kv_copy(3, kv_block(3, 0), 0, y_up),
        kv_copy(4, kv_block(1, 0), 1, y_down),
        kv_copy(5, kv_block(0, 1), None, y_up),
        kv_copy(6, kv_block(0, 1), None, y_down),
        kv_copy(7, kv_block(2, 0), None, partner),
    )
    kv_in = (
        kv_copy(0, kv_block(3, 0), None, y_up),
        kv_copy(1, kv_block(1, 0), None, y_down),
        kv_copy(2, kv_block(0, 1), None, partner),
        kv_copy(3, kv_block(2, 0), 0, y_up),
        kv_copy(4, kv_block(2, 0), 1, y_down),
        kv_copy(5, kv_block(3, 1), None, y_up),
        kv_copy(6, kv_block(1, 1), None, y_down),
        kv_copy(7, kv_block(2, 1), None, partner),
    )

    loads[0].wait()
    w_begin(0)
    loads[1].wait()
    loads[2].wait()
    for number in (0, 1, 2):
        kv_out[number].start()
    expert_loads = []
    for number, (src, dst) in enumerate(((gate_hbm, gate_w), (up_hbm, up_w), (down_hbm, down_w))):
        expert_loads.append(pltpu.make_async_copy(src, dst, expert_sem.at[number]))
        expert_loads[-1].start()

    loads[3].wait()
    loads[4].wait()
    shares = gates[...] / jnp.sum(gates[...], axis=0, keepdims=True)
    ids_here = ids[...]
    expert_row = lax.broadcasted_iota(jnp.int32, (EXPERTS, TOK), 0)
    dense = jnp.zeros((EXPERTS, TOK), jnp.float32)
    for k in range(TOPK):
        dense = dense + jnp.where(ids_here[k : k + 1] == expert_row, shares[k : k + 1], 0.0)
    for group in range(4):
        share_tiles[group] = dense[group * 8 : (group + 1) * 8]
    shares_in[exp] = share_tiles[exp // 4]
    share_sems = (share_send, share_recv)
    share_out, share_arrive = [], []
    for step in range(1, 16):
        there = lax.rem(exp + step, 16)
        behind = lax.rem(exp + 16 - step, 16)
        peer = {"ctx": ctx, "exp": there}
        tile = share_tiles.at[there // 4]
        share_out.append(send(tile, shares_in.at[exp], share_sems, step, peer))
        share_arrive.append(send(tile, shares_in.at[behind], share_sems, step, peer))

    w_end(0)
    w_begin(1)
    for copy in share_out:
        copy.start()
    for number in (0, 1, 2):
        kv_in[number].wait_recv()
    w_end(1)
    w_begin(2)
    for number in (3, 4, 5, 6):
        kv_out[number].start()
    kv_in[3].wait_recv()
    kv_in[4].wait_recv()
    kv_out[7].start()
    w_forward(0)
    for number in (5, 6, 7):
        kv_in[number].wait_recv()
    for copy in query_loads:
        copy.wait()

    att_sems = (att_send, att_recv)

    def att_copy(number):
        part = attended.at[core, :, pl.ds(pl.multiple_of(number * 512, 512), 512)]
        return send(part, part, att_sems, number, sibling)

    keys_total = 8 * TOK
    scale = HEAD_SIZE**-0.5 * 1.4426950408889634

    def heads(quad, carry):
        @pl.when(quad == 1)
        def _():
            w_forward(1)

        @pl.when(quad == 3)
        def _():
            w_forward(2)

        lanes = pl.ds(pl.multiple_of((quad // 2) * HEAD_SIZE, HEAD_SIZE), HEAD_SIZE)
        keys_here = jnp.concatenate([kv[block, 0, :, lanes] for block in range(8)], axis=0)
        values_here = jnp.concatenate([kv[block, 1, :, lanes] for block in range(8)], axis=0)
        values_wide = jnp.concatenate([values_here, jnp.ones_like(values_here)], axis=1)
        for part in range(4):
            scores = lax.dot_general(
                stacked[quad, part * TOK : (part + 1) * TOK],
                keys_here,
                (((1,), (1,)), ((), ())),
                preferred_element_type=jnp.float32,
            )
            query_at = lax.broadcasted_iota(jnp.int32, (TOK, keys_total), 0) + ctx * TOK
            key_at = lax.broadcasted_iota(jnp.int32, (TOK, keys_total), 1)
            scores = jnp.where(query_at >= key_at, scores, mask_fill_value)
            top = jnp.max(scores, axis=1, keepdims=True)
            weights = jnp.exp2((scores - top) * scale).astype(jnp.bfloat16)
            result = jnp.dot(weights, values_wide, preferred_element_type=jnp.float32)
            attended[
                core,
                :,
                pl.ds(pl.multiple_of(quad * 512 + part * HEAD_SIZE, HEAD_SIZE), HEAD_SIZE),
            ] = (result[:, :HEAD_SIZE] / result[:, HEAD_SIZE:]).astype(jnp.bfloat16)
        att_copy(quad).start()
        return carry

    lax.fori_loop(0, 8, heads, 0)

    for arriving in share_arrive:
        arriving.wait_recv()
    lane = lax.broadcasted_iota(jnp.int32, (TOK, TOK), 1)
    row = lax.broadcasted_iota(jnp.int32, (TOK, TOK), 0)
    up_to = (row <= lane).astype(jnp.float32).astype(jnp.bfloat16)
    slot_of_row = lax.rem(row, CAP).astype(jnp.float32)
    first_row = lax.rem(exp, 4) * 2

    def selection(block, carry):
        share_rows = jnp.concatenate(
            [
                jnp.broadcast_to(shares_in[block, pl.ds(first_row + j, 1)], (CAP, TOK))
                for j in range(2)
            ],
            axis=0,
        )
        chosen = share_rows > 0.0
        count = jnp.dot(
            chosen.astype(jnp.float32).astype(jnp.bfloat16),
            up_to,
            preferred_element_type=jnp.float32,
        )
        picked = chosen & (count - 1.0 == slot_of_row)
        pick[block] = picked.astype(jnp.float32).astype(jnp.bfloat16)
        scatter[block] = jnp.where(picked, share_rows, 0.0).T.astype(jnp.bfloat16)
        return carry

    lax.fori_loop(0, 16, selection, 0)

    for number in range(8):
        part = attended.at[other, :, pl.ds(number * 512, 512)]
        send(part, part, att_sems, number, sibling).wait_recv()
    w_end(2)

    def project(half, carry):
        rows = weight[half].reshape(8 * 512, 512)
        to_sibling[half] = jnp.dot(attended[other], rows, preferred_element_type=jnp.float32)
        from_sibling[2 + half] = jnp.dot(
            attended[core], rows, preferred_element_type=jnp.float32
        )
        return carry

    lax.fori_loop(0, 2, project, 0)
    swap = send(to_sibling, from_sibling.at[pl.ds(0, 2)], (proj_send, proj_recv), 0, sibling)
    swap.start()
    loads[5].wait()
    loads[6].wait()

    def place(first, which):
        for half in range(2):
            for depth in range(4):
                lanes = pl.ds(
                    pl.multiple_of(depth * 512 + half * 256 + which * 128, 128), 128
                )
                attn_resid_ref[:, lanes] = (
                    resid[:, lanes].astype(jnp.float32)
                    + from_sibling[first + half, :, depth * 128 : (depth + 1) * 128]
                ).astype(jnp.bfloat16)

    place(2, core)
    swap.wait_recv()
    place(0, other)
    wide = attn_resid_ref[...].astype(jnp.float32)
    scale_row = lax.rsqrt(jnp.mean(wide * wide, axis=1, keepdims=True) + norm_eps)
    blocks[exp] = (wide * scale_row * gain[...]).astype(jnp.bfloat16)

    def block_of(relation, which):
        dz, dx = RELATIONS[relation]
        return lax.rem(z + dz, 4) * 4 + lax.rem(x_high + dx, 2) * 2 + which

    ag = (ag_send, ag_recv)
    sib = (sib_send, sib_recv)
    low, high = pl.ds(0, CAP), pl.ds(CAP, CAP)

    def whole(relation):
        return blocks.at[block_of(relation, core)]

    def half_of(relation, rows):
        return blocks.at[block_of(relation, core), rows]

    ag_out = (
        send(whole(0), whole(0), ag, 0, z_up),
        send(whole(0), whole(0), ag, 1, z_down),
        send(whole(0), whole(0), ag, 2, x_over),
        send(half_of(1, low), half_of(1, low), ag, 3, z_up),
        send(half_of(2, high), half_of(2, high), ag, 4, z_down),
        send(whole(3), whole(3), ag, 5, z_up),
        send(whole(3), whole(3), ag, 6, z_down),
        send(whole(4), whole(4), ag, 7, x_over),
    )
    ag_in = (
        send(whole(1), whole(1), ag, 0, z_up),
        send(whole(2), whole(2), ag, 1, z_down),
        send(whole(3), whole(3), ag, 2, x_over),
        send(half_of(4, low), half_of(4, low), ag, 3, z_up),
        send(half_of(4, high), half_of(4, high), ag, 4, z_down),
        send(whole(5), whole(5), ag, 5, z_up),
        send(whole(6), whole(6), ag, 6, z_down),
        send(whole(7), whole(7), ag, 7, x_over),
    )
    sib_out = [send(whole(k), whole(k), sib, k, sibling) for k in range(8)]
    sib_in = []
    for k in range(8):
        arriving = blocks.at[block_of(k, other)]
        sib_in.append(send(arriving, arriving, sib, k, sibling))

    for number in (0, 1, 2):
        ag_out[number].start()
    sib_out[0].start()
    for copy in expert_loads:
        copy.wait()
    for piece in range(3):
        for stage in range(3):
            for copy in w_plan[piece][stage][0]:
                copy.wait_send()

    def part_of(block):
        return weight.at[block // 8, lax.rem(block // 4, 2), lax.rem(block, 4)]

    def part_rows(block, rows):
        return weight.at[block // 8, lax.rem(block // 4, 2), lax.rem(block, 4), rows]

    part = (part_send, part_recv)
    rs = (rs_send, rs_recv)
    left, right = pl.ds(0, 256), pl.ds(256, 256)
    both = pl.ds(0, 512)

    def part_copy(chip):
        return send(part_of(chip * 2 + other), sib_parts.at[chip], part, chip, sibling)

    def add_into(block, rows, extra):
        target = part_rows(block, rows)
        target[...] = (target[...].astype(jnp.float32) + extra[...].astype(jnp.float32)).astype(
            jnp.bfloat16
        )

    def chip_sum(relation):
        chip = block_of(relation, 0) // 2
        part_copy(chip).wait_recv()
        add_into(chip * 2 + core, both, sib_parts.at[chip])

    def toward(relation, rows):
        return part_rows(block_of(relation, core), rows)

    rs_out = (
        send(toward(7, left), hop_in.at[left], rs, 0, x_over),
        send(toward(7, right), hop_in.at[right], rs, 1, x_over),
        send(toward(5, both), full_in.at[2], rs, 2, z_down),
        send(toward(6, both), full_in.at[3], rs, 3, z_up),
        send(toward(1, right), full_in.at[0, right], rs, 4, z_down),
        send(toward(2, left), full_in.at[1, left], rs, 5, z_up),
        send(toward(4, left), half_in.at[0], rs, 6, z_down),
        send(toward(4, right), half_in.at[1], rs, 7, z_up),
        send(toward(3, both), far_in, rs, 8, x_over),
        send(toward(1, left), full_in.at[0, left], rs, 9, z_down),
        send(toward(2, right), full_in.at[1, right], rs, 10, z_up),
    )

    def step(number, carry):
        @pl.when(number == 0)
        def _():
            ag_in[0].wait_recv()
            ag_out[3].start()
            sib_out[1].start()
            ag_in[1].wait_recv()
            ag_out[4].start()
            sib_out[2].start()
            ag_in[2].wait_recv()
            ag_out[5].start()
            ag_out[6].start()
            sib_out[3].start()
            sib_in[0].wait_recv()
            sib_in[3].wait_recv()

        @pl.when(number == 1)
        def _():
            ag_in[3].wait_recv()
            ag_in[4].wait_recv()
            ag_out[7].start()
            sib_out[4].start()
            sib_in[1].wait_recv()
            sib_in[2].wait_recv()

        @pl.when(number == 2)
        def _():
            chip_sum(1)
            rs_out[4].start()
            chip_sum(2)
            rs_out[5].start()
            ag_in[5].wait_recv()
            sib_out[5].start()
            ag_in[6].wait_recv()
            sib_out[6].start()
            ag_in[7].wait_recv()
            sib_out[7].start()
            sib_in[4].wait_recv()
            sib_in[7].wait_recv()

        @pl.when(number == 3)
        def _():
            sib_in[5].wait_recv()
            sib_in[6].wait_recv()

        def chip_at(which):
            dz, dx = 0, 0
            for k, pair in enumerate(PAIRS):
                there = RELATIONS[pair[which]]
                dz = jnp.where(number == k, there[0], dz)
                dx = jnp.where(number == k, there[1], dx)
            return lax.rem(z + dz, 4) * 2 + lax.rem(x_high + dx, 2)

        chips = (chip_at(0), chip_at(1))
        sources = [chips[q // 2] * 2 + q % 2 for q in range(4)]
        for q in range(4):
            found = jnp.dot(
                pick[sources[q]], blocks[sources[q]], preferred_element_type=jnp.float32
            ).astype(jnp.bfloat16)
            for j in range(2):
                slots_in[j, q * CAP : (q + 1) * CAP] = found[j * CAP : (j + 1) * CAP]

        @pl.when(number == 3)
        def _():
            chip_sum(7)
            rs_out[0].start()
            rs_out[1].start()

        def expert(j, carry):
            for n in range(3):
                cols = slice(n * 256, (n + 1) * 256)
                gate_part = jnp.dot(
                    slots_in[j], gate_w[j, :, cols], preferred_element_type=jnp.float32
                )
                up_part = jnp.dot(
                    slots_in[j], up_w[j, :, cols], preferred_element_type=jnp.float32
                )
                act[:, cols] = (gate_part / (1.0 + jnp.exp(-gate_part)) * up_part).astype(
                    jnp.bfloat16
                )
            for n in range(4):
                cols = slice(n * 512, (n + 1) * 512)
                result = jnp.dot(act[...], down_w[j, :, cols], preferred_element_type=jnp.float32)
                for q in range(4):
                    slots_out[q, pl.ds(pl.multiple_of(j * CAP, CAP), CAP), cols] = result[
                        q * CAP : (q + 1) * CAP
                    ].astype(jnp.bfloat16)
            return carry

        lax.fori_loop(0, 2, expert, 0)
        for q in range(4):
            target = part_of(sources[q])
            for n in range(4):
                target[n * TOK : (n + 1) * TOK] = jnp.dot(
                    scatter[sources[q]],
                    slots_out[q, :, n * 512 : (n + 1) * 512],
                    preferred_element_type=jnp.float32,
                ).astype(jnp.bfloat16)
            if q % 2:
                part_copy(chips[q // 2]).start()
        return carry

    lax.fori_loop(0, 4, step, 0)

    chip_sum(5)
    rs_out[2].start()
    chip_sum(6)
    rs_out[3].start()
    chip_sum(4)
    rs_out[0].wait_recv()
    add_into(block_of(4, core), left, hop_in.at[left])
    rs_out[6].start()
    rs_out[1].wait_recv()
    add_into(block_of(4, core), right, hop_in.at[right])
    rs_out[7].start()
    chip_sum(3)
    chip_sum(0)
    rs_out[2].wait_recv()
    add_into(block_of(3, core), both, full_in.at[2])
    rs_out[3].wait_recv()
    add_into(block_of(3, core), both, full_in.at[3])
    rs_out[8].start()
    rs_out[6].wait_recv()
    add_into(block_of(1, core), left, half_in.at[0])
    rs_out[9].start()
    rs_out[7].wait_recv()
    add_into(block_of(2, core), right, half_in.at[1])
    rs_out[10].start()

    for number in (4, 5, 9, 10, 8):
        rs_out[number].wait_recv()
    for n in range(4):
        rows = slice(n * TOK, (n + 1) * TOK)
        cols = slice(n * 512, (n + 1) * 512)
        total = attn_resid_ref[:, cols].astype(jnp.float32)
        for extra in (part_of(exp), full_in.at[0], full_in.at[1], far_in):
            total = total + extra[rows].astype(jnp.float32)
        out_ref[:, cols] = total.astype(jnp.bfloat16)

    for copy in (*kv_out, *share_out, swap, *ag_out, *sib_out, *rs_out):
        copy.wait_send()
    for number in range(8):
        att_copy(number).wait_send()
        part_copy(number).wait_send()


def layer(*arrays):
    vmem = pl.BlockSpec(memory_space=pltpu.VMEM)
    hbm = pl.BlockSpec(memory_space=pl.ANY)
    dma = pltpu.SemaphoreType.DMA
    bf16, f32 = jnp.bfloat16, jnp.float32
    counts = (7, 32, 3, 8, 8, 36, 36, 16, 16, 8, 8, 1, 1, 8, 8, 8, 8, 8, 8, 11, 11)
    return pl.pallas_call(
        layer_kernel,
        out_shape=(
            jax.ShapeDtypeStruct((TOK, D), bf16),
            jax.ShapeDtypeStruct((TOK, D), bf16),
        ),
        in_specs=[hbm] * 11,
        out_specs=(vmem, vmem),
        scratch_shapes=[
            pltpu.VMEM((2, 2, 4, 512, 512), bf16),
            pltpu.VMEM((8, 2, TOK, 512), bf16),
            pltpu.VMEM((8, 512, HEAD_SIZE), bf16),
            pltpu.VMEM((2, TOK, 4096), bf16),
            pltpu.VMEM((2, TOK, 512), f32),
            pltpu.VMEM((4, TOK, 512), f32),
            pltpu.VMEM((TOK, D), bf16),
            pltpu.VMEM((1, D), f32),
            pltpu.VMEM((TOPK, TOK), jnp.int32),
            pltpu.VMEM((TOPK, TOK), f32),
            pltpu.VMEM((4, 8, TOK), f32),
            pltpu.VMEM((16, 8, TOK), f32),
            pltpu.VMEM((2, D, FF), bf16),
            pltpu.VMEM((2, D, FF), bf16),
            pltpu.VMEM((2, FF, D), bf16),
            pltpu.VMEM((16, TOK, D), bf16),
            pltpu.VMEM((8, 512, 512), bf16),
            pltpu.VMEM((2, 256, 512), bf16),
            pltpu.VMEM((4, 512, 512), bf16),
            pltpu.VMEM((512, 512), bf16),
            pltpu.VMEM((512, 512), bf16),
            pltpu.VMEM((2, 256, D), bf16),
            pltpu.VMEM((4, TOK, D), bf16),
            pltpu.VMEM((256, FF), bf16),
            pltpu.VMEM((16, TOK, TOK), bf16),
            pltpu.VMEM((16, TOK, TOK), bf16),
            *(dma((count,)) for count in counts),
        ],
        compiler_params=pltpu.CompilerParams(
            collective_id=0, has_side_effects=True, vmem_limit_bytes=62 << 20
        ),
    )(*arrays)


def local(
    queries,
    keys,
    values,
    resid,
    out_weight,
    norm_gain,
    expert_gate,
    expert_up,
    expert_down,
    route_ids,
    route_gates,
):
    attn_resid, layer_out = layer(
        queries[0],
        keys[0],
        values[0],
        resid[0],
        out_weight,
        norm_gain[None],
        route_ids[0].T,
        route_gates[0].T,
        expert_gate,
        expert_up,
        expert_down,
    )
    return (attn_resid[None], layer_out[None])


def solution(mesh):
    in_specs = (
        P("exp", "ctx", None),
        P("exp", "ctx", None),
        P("exp", "ctx", None),
        P("exp", "ctx", None),
        P("ctx", "exp"),
        P(),
        P("exp", None, None),
        P("exp", None, None),
        P("exp", None, None),
        P("exp", "ctx", None),
        P("exp", "ctx", None),
    )
    out_specs = (P("exp", "ctx", None), P("exp", "ctx", None))
    return jax.shard_map(local, mesh=mesh, in_specs=in_specs, out_specs=out_specs, check_vma=False)
```

time: 307 us -> 159 us (0.52)
  waiting for transfers between devices: 134 us -> 0 us
  Pallas kernels: 95.5 us -> 153 us
  starting transfers between devices: 19.8 us -> 0 us
  matrix products: 17.7 us -> 0 us
  between operations: 14.2 us -> 0.64 us
  local copies, waits for them, and re-layouts: 14.4 us -> 3.76 us
  other arithmetic: 9.04 us -> 0 us
    ppermute x7 -> x0, waiting for transfers between devices: 90.8 us -> none  [from_behind(): return lax.ppermute(shard, axis, pairs)]
    pallas_call x1, Pallas kernels: 95.5 us -> 153 us  [layer(): pl.pallas_call(layer_kernel, out_shape=(jax.ShapeDtypeStruct((TOK, D), bf...]
    all_gather x2 -> x0, waiting for transfers between devices: 42.1 us -> none  [the longest x1 42.1 us: local(): all_rows = lax.all_gather(out_weight, 'ctx', axis=0, tiled=True)]
    dot_general x11 -> x0, matrix products: 17.7 us -> none  [the longest x1 8.23 us: local(): jnp.dot(attention, lax.all_gather(all_rows, 'exp', axis=1, tiled=True), p...]
    ppermute x7 -> x0, starting transfers between devices: 13.4 us -> none  [from_behind(): return lax.ppermute(shard, axis, pairs)]
    while x8 -> x0, local copies, waits for them, and re-layouts: 6.79 us -> none
    all_to_all x1 -> x0, starting transfers between devices: 6.34 us -> none  [local(): lax.all_to_all(wanted, 'exp', split_axis=0, concat_axis=0, tiled=True)]
    reduce_sum x7 -> x0, other arithmetic: 4.19 us -> none  [the longest x5 2.77 us: attend_block(): row_total = row_total * factor + jnp.sum(exp_scores, axis=-1)]
  transfers between devices with their start and end apart: 10 -> 0, of which waited for: 8 -> 0; matrix products, arithmetic and copies ran while one was open for 13% -> 0% of each run, Pallas kernels for 0% -> 0%
where the time goes in v3:
time: 159 us; the launch traced here: 157 us
  Pallas kernels  153 us (96%)
  local copies, waits for them, and re-layouts  3.76 us (2%)
    pallas_call x1, Pallas kernels, layer(): pl.pallas_call(layer_kernel, out_shape=(jax.ShapeDtypeStruct((TOK, D), bf...  153 us
    unnamed x2, local copies, waits for them, and re-layouts  3.76 us

profile of v3, /device:TPU:2, one launch (start us, length us, event | category | flops | bytes accessed | tf_op | source)
XLA Modules:
  0.0 157.0 jit_solution(4134235115450986836)
XLA Ops:
  0.6 152.6 %shard_map.122 = (bf16[128,2048]{1,0:T(8,128)(2,1)}, bf16[128,2048]{1,0:T(8,128)(2,1)}) custom-call(bf16[128,4096]{1,0:T(8,128)(2,1)} %bitcast.13, bf16[128,512]{1,0:T(8,128)(2,1)} %bitcast.17, bf16[128,512]{1,0:T(8,128)(2,1)} %bitcast.18, bf16[128,2048]{1,0:T(8,128)(2,1)} %bitcast.14, bf16[512,128]{1,0:T(8,128)(2,1)} %weight_hbm.1, f32[1,2048]{1,0:T(1,128)} %bitcast.19, ...), custom_call_target="tpu_custom_call" | custom-call | tf_op jit(solution)/shard_map/pallas_call | solution.py:656
  153.2 1.9 %copy.15 = bf16[1,128,2048]{2,1,0:T(8,128)(2,1)} copy(bf16[1,128,2048]{2,1,0:T(8,128)(2,1)} %bitcast.16) | data formatting | bytes 1048576
  155.1 1.9 %copy.16 = bf16[1,128,2048]{2,1,0:T(8,128)(2,1)} copy(bf16[1,128,2048]{2,1,0:T(8,128)(2,1)} %bitcast.15) | data formatting | bytes 1048576

commit v4 on v3

--- a/solution.py
+++ b/solution.py
@@ -21,7 +21,7 @@
 mask_fill_value = -1e30
 
 RELATIONS = ((0, 0), (3, 0), (1, 0), (0, 1), (2, 0), (3, 1), (1, 1), (2, 1))
-PAIRS = ((0, 3), (1, 2), (4, 7), (5, 6))
+ORDER = (0, 1, 2, 3, 4, 7, 5, 6)
 PIECES = ((0, 208, 112, "xyz"), (208, 160, 80, "yzx"), (368, 144, 80, "zxy"))
 
 
@@ -285,14 +285,44 @@
         copy.start()
     for number in (0, 1, 2):
         kv_in[number].wait_recv()
+    for number in (3, 4, 5, 6):
+        kv_out[number].start()
     w_end(1)
     w_begin(2)
-    for number in (3, 4, 5, 6):
-        kv_out[number].start()
     kv_in[3].wait_recv()
     kv_in[4].wait_recv()
     kv_out[7].start()
-    w_forward(0)
+    for arriving in share_arrive:
+        arriving.wait_recv()
+    lane = lax.broadcasted_iota(jnp.int32, (TOK, TOK), 1)
+    row = lax.broadcasted_iota(jnp.int32, (TOK, TOK), 0)
+    up_to = (row <= lane).astype(jnp.float32).astype(jnp.bfloat16)
+    slot_of_row = lax.rem(row, CAP).astype(jnp.float32)
+    first_row = lax.rem(exp, 4) * 2
+
+    def selection(block, carry):
+        share_rows = jnp.concatenate(
+            [
+                jnp.broadcast_to(shares_in[block, pl.ds(first_row + j, 1)], (CAP, TOK))
+                for j in range(2)
+            ],
+            axis=0,
+        )
+        chosen = share_rows > 0.0
+        count = jnp.dot(
+            chosen.astype(jnp.float32).astype(jnp.bfloat16),
+            up_to,
+            preferred_element_type=jnp.float32,
+        )
+        picked = chosen & (count - 1.0 == slot_of_row)
+        pick[block] = picked.astype(jnp.float32).astype(jnp.bfloat16)
+        scatter[block] = jnp.where(picked, share_rows, 0.0).T.astype(jnp.bfloat16)
+        return carry
+
+    lax.fori_loop(0, 16, selection, 0)
+
+    for piece in range(3):
+        w_forward(piece)
     for number in (5, 6, 7):
         kv_in[number].wait_recv()
     for copy in query_loads:
@@ -308,14 +338,6 @@
     scale = HEAD_SIZE**-0.5 * 1.4426950408889634
 
     def heads(quad, carry):
-        @pl.when(quad == 1)
-        def _():
-            w_forward(1)
-
-        @pl.when(quad == 3)
-        def _():
-            w_forward(2)
-
         lanes = pl.ds(pl.multiple_of((quad // 2) * HEAD_SIZE, HEAD_SIZE), HEAD_SIZE)
         keys_here = jnp.concatenate([kv[block, 0, :, lanes] for block in range(8)], axis=0)
         values_here = jnp.concatenate([kv[block, 1, :, lanes] for block in range(8)], axis=0)
@@ -343,51 +365,27 @@
 
     lax.fori_loop(0, 8, heads, 0)
 
-    for arriving in share_arrive:
-        arriving.wait_recv()
-    lane = lax.broadcasted_iota(jnp.int32, (TOK, TOK), 1)
-    row = lax.broadcasted_iota(jnp.int32, (TOK, TOK), 0)
-    up_to = (row <= lane).astype(jnp.float32).astype(jnp.bfloat16)
-    slot_of_row = lax.rem(row, CAP).astype(jnp.float32)
-    first_row = lax.rem(exp, 4) * 2
-
-    def selection(block, carry):
-        share_rows = jnp.concatenate(
-            [
-                jnp.broadcast_to(shares_in[block, pl.ds(first_row + j, 1)], (CAP, TOK))
-                for j in range(2)
-            ],
-            axis=0,
-        )
-        chosen = share_rows > 0.0
-        count = jnp.dot(
-            chosen.astype(jnp.float32).astype(jnp.bfloat16),
-            up_to,
-            preferred_element_type=jnp.float32,
-        )
-        picked = chosen & (count - 1.0 == slot_of_row)
-        pick[block] = picked.astype(jnp.float32).astype(jnp.bfloat16)
-        scatter[block] = jnp.where(picked, share_rows, 0.0).T.astype(jnp.bfloat16)
-        return carry
-
-    lax.fori_loop(0, 16, selection, 0)
-
     for number in range(8):
         part = attended.at[other, :, pl.ds(number * 512, 512)]
         send(part, part, att_sems, number, sibling).wait_recv()
     w_end(2)
 
-    def project(half, carry):
-        rows = weight[half].reshape(8 * 512, 512)
-        to_sibling[half] = jnp.dot(attended[other], rows, preferred_element_type=jnp.float32)
-        from_sibling[2 + half] = jnp.dot(
-            attended[core], rows, preferred_element_type=jnp.float32
-        )
-        return carry
-
-    lax.fori_loop(0, 2, project, 0)
+    def project(whose):
+        def run(half, carry):
+            target, at = (to_sibling, half) if whose is other else (from_sibling, 2 + half)
+            target[at] = jnp.dot(
+                attended[whose],
+                weight[half].reshape(8 * 512, 512),
+                preferred_element_type=jnp.float32,
+            )
+            return carry
+
+        lax.fori_loop(0, 2, run, 0)
+
+    project(other)
     swap = send(to_sibling, from_sibling.at[pl.ds(0, 2)], (proj_send, proj_recv), 0, sibling)
     swap.start()
+    project(core)
     loads[5].wait()
     loads[6].wait()
 
@@ -423,33 +421,37 @@
     def half_of(relation, rows):
         return blocks.at[block_of(relation, core), rows]
 
-    ag_out = (
-        send(whole(0), whole(0), ag, 0, z_up),
-        send(whole(0), whole(0), ag, 1, z_down),
-        send(whole(0), whole(0), ag, 2, x_over),
-        send(half_of(1, low), half_of(1, low), ag, 3, z_up),
-        send(half_of(2, high), half_of(2, high), ag, 4, z_down),
-        send(whole(3), whole(3), ag, 5, z_up),
-        send(whole(3), whole(3), ag, 6, z_down),
-        send(whole(4), whole(4), ag, 7, x_over),
+    quarters = [pl.ds(n * 32, 32) for n in range(4)]
+    z_moves = (
+        (0, low, 1, z_up),
+        (0, high, 2, z_down),
+        (0, None, 3, x_over),
+        (0, high, 1, z_up),
+        (0, low, 2, z_down),
+        (1, quarters[0], 4, z_up),
+        (2, quarters[2], 4, z_down),
+        (1, quarters[1], 4, z_up),
+        (2, quarters[3], 4, z_down),
+        (3, None, 5, z_up),
+        (3, None, 6, z_down),
+        (4, quarters[0], 7, x_over),
+        (4, quarters[2], 7, x_over),
+        (4, quarters[1], 7, x_over),
+        (4, quarters[3], 7, x_over),
     )
-    ag_in = (
-        send(whole(1), whole(1), ag, 0, z_up),
-        send(whole(2), whole(2), ag, 1, z_down),
-        send(whole(3), whole(3), ag, 2, x_over),
-        send(half_of(4, low), half_of(4, low), ag, 3, z_up),
-        send(half_of(4, high), half_of(4, high), ag, 4, z_down),
-        send(whole(5), whole(5), ag, 5, z_up),
-        send(whole(6), whole(6), ag, 6, z_down),
-        send(whole(7), whole(7), ag, 7, x_over),
-    )
+    ag_out, ag_in = [], []
+    for number, (sent, rows, got, peer) in enumerate(z_moves):
+        mine = whole(sent) if rows is None else half_of(sent, rows)
+        theirs = whole(got) if rows is None else half_of(got, rows)
+        ag_out.append(send(mine, mine, ag, number, peer))
+        ag_in.append(send(theirs, theirs, ag, number, peer))
     sib_out = [send(whole(k), whole(k), sib, k, sibling) for k in range(8)]
     sib_in = []
     for k in range(8):
         arriving = blocks.at[block_of(k, other)]
         sib_in.append(send(arriving, arriving, sib, k, sibling))
 
-    for number in (0, 1, 2):
+    for number in range(5):
         ag_out[number].start()
     sib_out[0].start()
     for copy in expert_loads:
@@ -487,87 +489,112 @@
     def toward(relation, rows):
         return part_rows(block_of(relation, core), rows)
 
-    rs_out = (
-        send(toward(7, left), hop_in.at[left], rs, 0, x_over),
-        send(toward(7, right), hop_in.at[right], rs, 1, x_over),
-        send(toward(5, both), full_in.at[2], rs, 2, z_down),
-        send(toward(6, both), full_in.at[3], rs, 3, z_up),
-        send(toward(1, right), full_in.at[0, right], rs, 4, z_down),
-        send(toward(2, left), full_in.at[1, left], rs, 5, z_up),
-        send(toward(4, left), half_in.at[0], rs, 6, z_down),
-        send(toward(4, right), half_in.at[1], rs, 7, z_up),
-        send(toward(3, both), far_in, rs, 8, x_over),
-        send(toward(1, left), full_in.at[0, left], rs, 9, z_down),
-        send(toward(2, right), full_in.at[1, right], rs, 10, z_up),
-    )
+    fourths = [pl.ds(n * TOK, TOK) for n in range(4)]
+    rs_out = [send(toward(7, rows), hop_in.at[rows], rs, n, x_over) for n, rows in enumerate(fourths)]
+    rs_out.append(send(toward(5, left), full_in.at[2, left], rs, 4, z_down))
+    rs_out.append(send(toward(5, right), full_in.at[2, right], rs, 5, z_down))
+    rs_out.append(send(toward(6, left), full_in.at[3, left], rs, 6, z_up))
+    rs_out.append(send(toward(6, right), full_in.at[3, right], rs, 7, z_up))
+    rs_out.append(send(toward(1, right), full_in.at[0, right], rs, 8, z_down))
+    rs_out.append(send(toward(2, left), full_in.at[1, left], rs, 9, z_up))
+    for n, rows in enumerate(fourths):
+        into = half_in.at[n // 2, pl.ds(n % 2 * TOK, TOK)]
+        rs_out.append(send(toward(4, rows), into, rs, 10 + n, (z_down, z_up)[n // 2]))
+    for n, rows in enumerate(fourths):
+        into = full_in.at[n // 2, rows]
+        rs_out.append(send(toward(1 + n // 2, rows), into, rs, 14 + n, (z_down, z_up)[n // 2]))
+    rs_out.append(send(toward(3, left), far_in.at[left], rs, 18, x_over))
+    rs_out.append(send(toward(3, right), far_in.at[right], rs, 19, x_over))
 
     def step(number, carry):
         @pl.when(number == 0)
         def _():
+            sib_in[0].wait_recv()
+
+        @pl.when(number == 1)
+        def _():
             ag_in[0].wait_recv()
-            ag_out[3].start()
+            ag_out[5].start()
+            ag_out[7].start()
+            ag_in[1].wait_recv()
+            ag_out[6].start()
+            ag_out[8].start()
+            ag_in[3].wait_recv()
             sib_out[1].start()
-            ag_in[1].wait_recv()
-            ag_out[4].start()
+            ag_in[4].wait_recv()
             sib_out[2].start()
             ag_in[2].wait_recv()
-            ag_out[5].start()
-            ag_out[6].start()
             sib_out[3].start()
-            sib_in[0].wait_recv()
+            sib_in[1].wait_recv()
+
+        @pl.when(number == 2)
+        def _():
+            for k in (5, 6):
+                ag_in[k].wait_recv()
+                ag_out[k + 6].start()
+            ag_out[9].start()
+            ag_out[10].start()
+            sib_in[2].wait_recv()
+
+        @pl.when(number == 3)
+        def _():
+            for k in (7, 8):
+                ag_in[k].wait_recv()
+                ag_out[k + 6].start()
+            sib_out[4].start()
             sib_in[3].wait_recv()
 
-        @pl.when(number == 1)
-        def _():
-            ag_in[3].wait_recv()
-            ag_in[4].wait_recv()
-            ag_out[7].start()
-            sib_out[4].start()
-            sib_in[1].wait_recv()
-            sib_in[2].wait_recv()
-
-        @pl.when(number == 2)
+        @pl.when(number == 4)
+        def _():
+            sib_in[4].wait_recv()
+
+        @pl.when(number == 5)
         def _():
             chip_sum(1)
-            rs_out[4].start()
             chip_sum(2)
-            rs_out[5].start()
-            ag_in[5].wait_recv()
+            ag_in[9].wait_recv()
             sib_out[5].start()
-            ag_in[6].wait_recv()
+            ag_in[10].wait_recv()
             sib_out[6].start()
-            ag_in[7].wait_recv()
+            rs_out[8].start()
+            rs_out[9].start()
+            for k in (11, 12, 13, 14):
+                ag_in[k].wait_recv()
             sib_out[7].start()
-            sib_in[4].wait_recv()
             sib_in[7].wait_recv()
 
-        @pl.when(number == 3)
+        @pl.when(number == 6)
         def _():
             sib_in[5].wait_recv()
+
+        @pl.when(number == 7)
+        def _():
             sib_in[6].wait_recv()
 
-        def chip_at(which):
-            dz, dx = 0, 0
-            for k, pair in enumerate(PAIRS):
-                there = RELATIONS[pair[which]]
-                dz = jnp.where(number == k, there[0], dz)
-                dx = jnp.where(number == k, there[1], dx)
-            return lax.rem(z + dz, 4) * 2 + lax.rem(x_high + dx, 2)
-
-        chips = (chip_at(0), chip_at(1))
-        sources = [chips[q // 2] * 2 + q % 2 for q in range(4)]
-        for q in range(4):
+        dz, dx = 0, 0
+        for k, relation in enumerate(ORDER):
+            dz = jnp.where(number == k, RELATIONS[relation][0], dz)
+            dx = jnp.where(number == k, RELATIONS[relation][1], dx)
+        chip = lax.rem(z + dz, 4) * 2 + lax.rem(x_high + dx, 2)
+        for q in range(2):
             found = jnp.dot(
-                pick[sources[q]], blocks[sources[q]], preferred_element_type=jnp.float32
+                pick[chip * 2 + q], blocks[chip * 2 + q], preferred_element_type=jnp.float32
             ).astype(jnp.bfloat16)
             for j in range(2):
                 slots_in[j, q * CAP : (q + 1) * CAP] = found[j * CAP : (j + 1) * CAP]
 
-        @pl.when(number == 3)
+        @pl.when(number == 6)
         def _():
             chip_sum(7)
-            rs_out[0].start()
-            rs_out[1].start()
+            for n in (0, 2, 1, 3):
+                rs_out[n].start()
+            chip_sum(4)
+
+        @pl.when(number == 7)
+        def _():
+            chip_sum(5)
+            rs_out[4].start()
+            rs_out[5].start()
 
         def expert(j, carry):
             for n in range(3):
@@ -584,57 +611,70 @@
             for n in range(4):
                 cols = slice(n * 512, (n + 1) * 512)
                 result = jnp.dot(act[...], down_w[j, :, cols], preferred_element_type=jnp.float32)
-                for q in range(4):
+                for q in range(2):
                     slots_out[q, pl.ds(pl.multiple_of(j * CAP, CAP), CAP), cols] = result[
                         q * CAP : (q + 1) * CAP
                     ].astype(jnp.bfloat16)
             return carry
 
         lax.fori_loop(0, 2, expert, 0)
-        for q in range(4):
-            target = part_of(sources[q])
+        for which in (other, core):
+            target = part_of(chip * 2 + which)
             for n in range(4):
                 target[n * TOK : (n + 1) * TOK] = jnp.dot(
-                    scatter[sources[q]],
-                    slots_out[q, :, n * 512 : (n + 1) * 512],
+                    scatter[chip * 2 + which],
+                    slots_out[which, :, n * 512 : (n + 1) * 512],
                     preferred_element_type=jnp.float32,
                 ).astype(jnp.bfloat16)
-            if q % 2:
-                part_copy(chips[q // 2]).start()
+            if which is other:
+                part_copy(chip).start()
         return carry
 
-    lax.fori_loop(0, 4, step, 0)
-
-    chip_sum(5)
-    rs_out[2].start()
+    lax.fori_loop(0, 8, step, 0)
+
     chip_sum(6)
-    rs_out[3].start()
-    chip_sum(4)
-    rs_out[0].wait_recv()
-    add_into(block_of(4, core), left, hop_in.at[left])
     rs_out[6].start()
-    rs_out[1].wait_recv()
-    add_into(block_of(4, core), right, hop_in.at[right])
     rs_out[7].start()
+
+    def opposite(n):
+        rs_out[n].wait_recv()
+        add_into(block_of(4, core), fourths[n], hop_in.at[fourths[n]])
+        rs_out[10 + n].start()
+
+    def beside(n):
+        rs_out[10 + n].wait_recv()
+        into = half_in.at[n // 2, pl.ds(n % 2 * TOK, TOK)]
+        add_into(block_of(1 + n // 2, core), fourths[n], into)
+        rs_out[14 + n].start()
+
+    def across(n, rows):
+        rs_out[4 + n].wait_recv()
+        add_into(block_of(3, core), rows, full_in.at[2, rows])
+        rs_out[6 + n].wait_recv()
+        add_into(block_of(3, core), rows, full_in.at[3, rows])
+        rs_out[18 + n].start()
+
+    opposite(0)
+    opposite(2)
     chip_sum(3)
+    opposite(1)
     chip_sum(0)
-    rs_out[2].wait_recv()
-    add_into(block_of(3, core), both, full_in.at[2])
-    rs_out[3].wait_recv()
-    add_into(block_of(3, core), both, full_in.at[3])
-    rs_out[8].start()
-    rs_out[6].wait_recv()
-    add_into(block_of(1, core), left, half_in.at[0])
-    rs_out[9].start()
-    rs_out[7].wait_recv()
-    add_into(block_of(2, core), right, half_in.at[1])
-    rs_out[10].start()
-
-    for number in (4, 5, 9, 10, 8):
-        rs_out[number].wait_recv()
+    opposite(3)
+    beside(0)
+    beside(2)
+    across(0, left)
+    beside(1)
+    beside(3)
+    across(1, right)
+
+    rs_out[8].wait_recv()
+    rs_out[9].wait_recv()
     for n in range(4):
         rows = slice(n * TOK, (n + 1) * TOK)
         cols = slice(n * 512, (n + 1) * 512)
+        rs_out[14 + n].wait_recv()
+        if n % 2 == 0:
+            rs_out[18 + n // 2].wait_recv()
         total = attn_resid_ref[:, cols].astype(jnp.float32)
         for extra in (part_of(exp), full_in.at[0], full_in.at[1], far_in):
             total = total + extra[rows].astype(jnp.float32)
@@ -652,7 +692,7 @@
     hbm = pl.BlockSpec(memory_space=pl.ANY)
     dma = pltpu.SemaphoreType.DMA
     bf16, f32 = jnp.bfloat16, jnp.float32
-    counts = (7, 32, 3, 8, 8, 36, 36, 16, 16, 8, 8, 1, 1, 8, 8, 8, 8, 8, 8, 11, 11)
+    counts = (7, 32, 3, 8, 8, 36, 36, 16, 16, 8, 8, 1, 1, 15, 15, 8, 8, 8, 8, 20, 20)
     return pl.pallas_call(
         layer_kernel,
         out_shape=(
@@ -683,9 +723,9 @@
             pltpu.VMEM((4, 512, 512), bf16),
             pltpu.VMEM((512, 512), bf16),
             pltpu.VMEM((512, 512), bf16),
-            pltpu.VMEM((2, 256, D), bf16),
-            pltpu.VMEM((4, TOK, D), bf16),
-            pltpu.VMEM((256, FF), bf16),
+            pltpu.VMEM((2, TOK, D), bf16),
+            pltpu.VMEM((2, TOK, D), bf16),
+            pltpu.VMEM((TOK, FF), bf16),
             pltpu.VMEM((16, TOK, TOK), bf16),
             pltpu.VMEM((16, TOK, TOK), bf16),
             *(dma((count,)) for count in counts),

time: 159 us -> 155 us (0.975)
  Pallas kernels: 153 us -> 148 us
    pallas_call x1, Pallas kernels: 153 us -> 148 us  [layer(): pl.pallas_call(layer_kernel, out_shape=(jax.ShapeDtypeStruct((TOK, D), bf...]
where the time goes in v4:
time: 155 us; the launch traced here: 152 us
  Pallas kernels  148 us (95%)
  local copies, waits for them, and re-layouts  3.76 us (2%)
    pallas_call x1, Pallas kernels, layer(): pl.pallas_call(layer_kernel, out_shape=(jax.ShapeDtypeStruct((TOK, D), bf...  148 us
    unnamed x2, local copies, waits for them, and re-layouts  3.76 us

profile of v4, /device:TPU:2, one launch (start us, length us, event | category | flops | bytes accessed | tf_op | source)
XLA Modules:
  0.0 152.2 jit_solution(14916298824757091522)
XLA Ops:
  0.6 147.8 %shard_map.122 = (bf16[128,2048]{1,0:T(8,128)(2,1)}, bf16[128,2048]{1,0:T(8,128)(2,1)}) custom-call(bf16[128,4096]{1,0:T(8,128)(2,1)} %bitcast.13, bf16[128,512]{1,0:T(8,128)(2,1)} %bitcast.17, bf16[128,512]{1,0:T(8,128)(2,1)} %bitcast.18, bf16[128,2048]{1,0:T(8,128)(2,1)} %bitcast.14, bf16[512,128]{1,0:T(8,128)(2,1)} %weight_hbm.1, f32[1,2048]{1,0:T(1,128)} %bitcast.19, ...), custom_call_target="tpu_custom_call" | custom-call | tf_op jit(solution)/shard_map/pallas_call | solution.py:696
  148.5 1.9 %copy.15 = bf16[1,128,2048]{2,1,0:T(8,128)(2,1)} copy(bf16[1,128,2048]{2,1,0:T(8,128)(2,1)} %bitcast.16) | data formatting | bytes 1048576
  150.3 1.9 %copy.16 = bf16[1,128,2048]{2,1,0:T(8,128)(2,1)} copy(bf16[1,128,2048]{2,1,0:T(8,128)(2,1)} %bitcast.15) | data formatting | bytes 1048576

commit v5 on v4

--- a/solution.py
+++ b/solution.py
@@ -37,8 +37,7 @@
     gate_hbm,
     up_hbm,
     down_hbm,
-    attn_resid_ref,
-    out_ref,
+    outs_ref,
     weight,
     kv,
     stacked,
@@ -87,6 +86,7 @@
     rs_send,
     rs_recv,
 ):
+    attn_resid_ref, out_ref = outs_ref.at[0], outs_ref.at[1]
     ctx, exp = lax.axis_index("ctx"), lax.axis_index("exp")
     x_low, y = ctx // 4, lax.rem(ctx, 4)
     z, x_high, core = exp // 4, lax.rem(exp // 2, 2), lax.rem(exp, 2)
@@ -490,21 +490,49 @@
         return part_rows(block_of(relation, core), rows)
 
     fourths = [pl.ds(n * TOK, TOK) for n in range(4)]
-    rs_out = [send(toward(7, rows), hop_in.at[rows], rs, n, x_over) for n, rows in enumerate(fourths)]
-    rs_out.append(send(toward(5, left), full_in.at[2, left], rs, 4, z_down))
-    rs_out.append(send(toward(5, right), full_in.at[2, right], rs, 5, z_down))
-    rs_out.append(send(toward(6, left), full_in.at[3, left], rs, 6, z_up))
-    rs_out.append(send(toward(6, right), full_in.at[3, right], rs, 7, z_up))
-    rs_out.append(send(toward(1, right), full_in.at[0, right], rs, 8, z_down))
-    rs_out.append(send(toward(2, left), full_in.at[1, left], rs, 9, z_up))
+    rs_out = []
+
+    def rs_send_rows(relation, rows, into, peer):
+        rs_out.append(send(toward(relation, rows), into, rs, len(rs_out), peer))
+
+    def quarter_in(n):
+        return half_in.at[n // 2, pl.ds(n % 2 * TOK, TOK)]
+
+    z_way = (z_down, z_down, z_up, z_up)
     for n, rows in enumerate(fourths):
-        into = half_in.at[n // 2, pl.ds(n % 2 * TOK, TOK)]
-        rs_out.append(send(toward(4, rows), into, rs, 10 + n, (z_down, z_up)[n // 2]))
+        rs_send_rows(4, rows, quarter_in(n), z_way[n])
+    rs_send_rows(1, right, full_in.at[0, right], z_down)
+    rs_send_rows(2, left, full_in.at[1, left], z_up)
     for n, rows in enumerate(fourths):
-        into = full_in.at[n // 2, rows]
-        rs_out.append(send(toward(1 + n // 2, rows), into, rs, 14 + n, (z_down, z_up)[n // 2]))
-    rs_out.append(send(toward(3, left), far_in.at[left], rs, 18, x_over))
-    rs_out.append(send(toward(3, right), far_in.at[right], rs, 19, x_over))
+        rs_send_rows(1 + n // 2, rows, full_in.at[n // 2, rows], z_way[n])
+    for n, rows in enumerate(fourths):
+        rs_send_rows(7, rows, hop_in.at[rows], z_way[n])
+    rs_send_rows(5, right, full_in.at[2, right], z_down)
+    rs_send_rows(6, left, full_in.at[3, left], z_up)
+    for n, rows in enumerate(fourths):
+        rs_send_rows(5 + n // 2, rows, full_in.at[2 + n // 2, rows], z_way[n])
+    for rows in fourths:
+        rs_send_rows(3, rows, far_in.at[rows], x_over)
+
+    def beside(n):
+        rs_out[n].wait_recv()
+        add_into(block_of(1 + n // 2, core), fourths[n], quarter_in(n))
+        rs_out[6 + n].start()
+
+    def beside_other(n):
+        rs_out[10 + n].wait_recv()
+        add_into(block_of(5 + n // 2, core), fourths[n], hop_in.at[fourths[n]])
+        rs_out[16 + n].start()
+
+    def across(n):
+        rs_out[16 + n].wait_recv()
+        target = toward(3, fourths[n])
+        target[...] = (
+            target[...].astype(jnp.float32)
+            + full_in[2, fourths[n]].astype(jnp.float32)
+            + full_in[3, fourths[n]].astype(jnp.float32)
+        ).astype(jnp.bfloat16)
+        rs_out[20 + n].start()
 
     def step(number, carry):
         @pl.when(number == 0)
@@ -556,8 +584,9 @@
             sib_out[5].start()
             ag_in[10].wait_recv()
             sib_out[6].start()
-            rs_out[8].start()
-            rs_out[9].start()
+            chip_sum(4)
+            for n in (0, 2, 1, 3, 4, 5):
+                rs_out[n].start()
             for k in (11, 12, 13, 14):
                 ag_in[k].wait_recv()
             sib_out[7].start()
@@ -587,14 +616,16 @@
         def _():
             chip_sum(7)
             for n in (0, 2, 1, 3):
-                rs_out[n].start()
-            chip_sum(4)
+                rs_out[10 + n].start()
+            beside(0)
+            beside(2)
 
         @pl.when(number == 7)
         def _():
             chip_sum(5)
-            rs_out[4].start()
-            rs_out[5].start()
+            rs_out[14].start()
+            beside(1)
+            beside(3)
 
         def expert(j, carry):
             for n in range(3):
@@ -633,48 +664,25 @@
     lax.fori_loop(0, 8, step, 0)
 
     chip_sum(6)
-    rs_out[6].start()
-    rs_out[7].start()
-
-    def opposite(n):
-        rs_out[n].wait_recv()
-        add_into(block_of(4, core), fourths[n], hop_in.at[fourths[n]])
-        rs_out[10 + n].start()
-
-    def beside(n):
-        rs_out[10 + n].wait_recv()
-        into = half_in.at[n // 2, pl.ds(n % 2 * TOK, TOK)]
-        add_into(block_of(1 + n // 2, core), fourths[n], into)
-        rs_out[14 + n].start()
-
-    def across(n, rows):
-        rs_out[4 + n].wait_recv()
-        add_into(block_of(3, core), rows, full_in.at[2, rows])
-        rs_out[6 + n].wait_recv()
-        add_into(block_of(3, core), rows, full_in.at[3, rows])
-        rs_out[18 + n].start()
-
-    opposite(0)
-    opposite(2)
+    rs_out[15].start()
+    for n in (0, 2, 1, 3):
+        beside_other(n)
     chip_sum(3)
-    opposite(1)
     chip_sum(0)
-    opposite(3)
-    beside(0)
-    beside(2)
-    across(0, left)
-    beside(1)
-    beside(3)
-    across(1, right)
-
-    rs_out[8].wait_recv()
-    rs_out[9].wait_recv()
-    for n in range(4):
+    rs_out[15].wait_recv()
+    across(0)
+    rs_out[14].wait_recv()
+    across(2)
+    across(1)
+    across(3)
+
+    rs_out[4].wait_recv()
+    rs_out[5].wait_recv()
+    for n in (0, 2, 1, 3):
         rows = slice(n * TOK, (n + 1) * TOK)
         cols = slice(n * 512, (n + 1) * 512)
-        rs_out[14 + n].wait_recv()
-        if n % 2 == 0:
-            rs_out[18 + n // 2].wait_recv()
+        rs_out[6 + n].wait_recv()
+        rs_out[20 + n].wait_recv()
         total = attn_resid_ref[:, cols].astype(jnp.float32)
         for extra in (part_of(exp), full_in.at[0], full_in.at[1], far_in):
             total = total + extra[rows].astype(jnp.float32)
@@ -692,15 +700,12 @@
     hbm = pl.BlockSpec(memory_space=pl.ANY)
     dma = pltpu.SemaphoreType.DMA
     bf16, f32 = jnp.bfloat16, jnp.float32
-    counts = (7, 32, 3, 8, 8, 36, 36, 16, 16, 8, 8, 1, 1, 15, 15, 8, 8, 8, 8, 20, 20)
+    counts = (7, 32, 3, 8, 8, 36, 36, 16, 16, 8, 8, 1, 1, 15, 15, 8, 8, 8, 8, 24, 24)
     return pl.pallas_call(
         layer_kernel,
-        out_shape=(
-            jax.ShapeDtypeStruct((TOK, D), bf16),
-            jax.ShapeDtypeStruct((TOK, D), bf16),
-        ),
+        out_shape=jax.ShapeDtypeStruct((2, TOK, D), bf16),
         in_specs=[hbm] * 11,
-        out_specs=(vmem, vmem),
+        out_specs=vmem,
         scratch_shapes=[
             pltpu.VMEM((2, 2, 4, 512, 512), bf16),
             pltpu.VMEM((8, 2, TOK, 512), bf16),
@@ -749,7 +754,7 @@
     route_ids,
     route_gates,
 ):
-    attn_resid, layer_out = layer(
+    outs = layer(
         queries[0],
         keys[0],
         values[0],
@@ -762,7 +767,7 @@
         expert_up,
         expert_down,
     )
-    return (attn_resid[None], layer_out[None])
+    return (outs[0][None], outs[1][None])
 
 
 def solution(mesh):

time: 155 us -> 149 us (0.961); the launches traced: 152 us -> 149 us
  Pallas kernels: 148 us -> 146 us
    unnamed x2 -> x0, local copies, waits for them, and re-layouts: 3.76 us -> none
    slice x0 -> x1, local copies, waits for them, and re-layouts: none -> 2.28 us  [local(): return (outs[0][None], outs[1][None])]
    pallas_call x1, Pallas kernels: 148 us -> 146 us  [layer(): pl.pallas_call(layer_kernel, out_shape=jax.ShapeDtypeStruct((2, TOK, D),...]
where the time goes in v5:
time: 149 us
  Pallas kernels  146 us (98%)
  local copies, waits for them, and re-layouts  2.28 us (2%)
    pallas_call x1, Pallas kernels, layer(): pl.pallas_call(layer_kernel, out_shape=jax.ShapeDtypeStruct((2, TOK, D),...  146 us

profile of v5, /device:TPU:2, one launch (start us, length us, event | category | flops | bytes accessed | tf_op | source)
XLA Modules:
  0.0 148.7 jit_solution(16267573746490584295)
XLA Ops:
  0.6 145.8 %shard_map.122 = bf16[2,128,2048]{2,1,0:T(8,128)(2,1)} custom-call(bf16[128,4096]{1,0:T(8,128)(2,1)} %bitcast.11, bf16[128,512]{1,0:T(8,128)(2,1)} %bitcast.13, bf16[128,512]{1,0:T(8,128)(2,1)} %bitcast.14, bf16[128,2048]{1,0:T(8,128)(2,1)} %bitcast.12, bf16[512,128]{1,0:T(8,128)(2,1)} %weight_hbm.1, f32[1,2048]{1,0:T(1,128)} %bitcast.15, ...), custom_call_target="tpu_custom_call" | custom-call | tf_op jit(solution)/shard_map/pallas_call | solution.py:704
  146.4 2.3 %fusion = (bf16[1,128,2048]{2,1,0:T(8,128)(2,1)}, bf16[1,128,2048]{2,1,0:T(8,128)(2,1)}) fusion(bf16[2,128,2048]{2,1,0:T(8,128)(2,1)} %shard_map.122), kind=kLoop, calls=%fused_computation | loop fusion | bytes 2097152 | tf_op jit(solution)/shard_map/slice | solution.py:770

commit v6 on v5

--- a/solution.py
+++ b/solution.py
@@ -22,7 +22,7 @@
 
 RELATIONS = ((0, 0), (3, 0), (1, 0), (0, 1), (2, 0), (3, 1), (1, 1), (2, 1))
 ORDER = (0, 1, 2, 3, 4, 7, 5, 6)
-PIECES = ((0, 208, 112, "xyz"), (208, 160, 80, "yzx"), (368, 144, 80, "zxy"))
+PIECES = ((0, 192, 96, "yxz"), (192, 160, 80, "zyx"), (352, 160, 80, "xzy"))
 
 
 def layer_kernel(
@@ -59,6 +59,7 @@
     full_in,
     far_in,
     hop_in,
+    x_in,
     slots_in,
     slots_out,
     act,
@@ -501,18 +502,22 @@
     z_way = (z_down, z_down, z_up, z_up)
     for n, rows in enumerate(fourths):
         rs_send_rows(4, rows, quarter_in(n), z_way[n])
-    rs_send_rows(1, right, full_in.at[0, right], z_down)
-    rs_send_rows(2, left, full_in.at[1, left], z_up)
+    rs_send_rows(1, fourths[2], full_in.at[0, fourths[2]], z_down)
+    rs_send_rows(2, fourths[1], full_in.at[1, fourths[1]], z_up)
     for n, rows in enumerate(fourths):
         rs_send_rows(1 + n // 2, rows, full_in.at[n // 2, rows], z_way[n])
     for n, rows in enumerate(fourths):
         rs_send_rows(7, rows, hop_in.at[rows], z_way[n])
-    rs_send_rows(5, right, full_in.at[2, right], z_down)
-    rs_send_rows(6, left, full_in.at[3, left], z_up)
+    rs_send_rows(5, fourths[2], full_in.at[2, fourths[2]], z_down)
+    rs_send_rows(6, fourths[1], full_in.at[3, fourths[1]], z_up)
     for n, rows in enumerate(fourths):
         rs_send_rows(5 + n // 2, rows, full_in.at[2 + n // 2, rows], z_way[n])
     for rows in fourths:
         rs_send_rows(3, rows, far_in.at[rows], x_over)
+    rs_send_rows(5, fourths[3], x_in.at[0], x_over)
+    rs_send_rows(6, fourths[0], x_in.at[1], x_over)
+    rs_send_rows(1, fourths[3], full_in.at[0, fourths[3]], z_down)
+    rs_send_rows(2, fourths[0], full_in.at[1, fourths[0]], z_up)
 
     def beside(n):
         rs_out[n].wait_recv()
@@ -524,15 +529,20 @@
         add_into(block_of(5 + n // 2, core), fourths[n], hop_in.at[fourths[n]])
         rs_out[16 + n].start()
 
-    def across(n):
-        rs_out[16 + n].wait_recv()
+    def across(n, which, numbers):
+        for number in numbers:
+            rs_out[number].wait_recv()
         target = toward(3, fourths[n])
-        target[...] = (
-            target[...].astype(jnp.float32)
-            + full_in[2, fourths[n]].astype(jnp.float32)
-            + full_in[3, fourths[n]].astype(jnp.float32)
-        ).astype(jnp.bfloat16)
+        total = target[...].astype(jnp.float32)
+        for k in which:
+            total = total + full_in[k, fourths[n]].astype(jnp.float32)
+        target[...] = total.astype(jnp.bfloat16)
         rs_out[20 + n].start()
+
+    def joined(k):
+        rs_out[24 + k].wait_recv()
+        add_into(block_of(1 + k, core), fourths[3 - 3 * k], x_in.at[k])
+        rs_out[26 + k].start()
 
     def step(number, carry):
         @pl.when(number == 0)
@@ -624,6 +634,7 @@
         def _():
             chip_sum(5)
             rs_out[14].start()
+            rs_out[24].start()
             beside(1)
             beside(3)
 
@@ -664,25 +675,25 @@
     lax.fori_loop(0, 8, step, 0)
 
     chip_sum(6)
+    rs_out[25].start()
     rs_out[15].start()
     for n in (0, 2, 1, 3):
         beside_other(n)
     chip_sum(3)
     chip_sum(0)
-    rs_out[15].wait_recv()
-    across(0)
-    rs_out[14].wait_recv()
-    across(2)
-    across(1)
-    across(3)
-
-    rs_out[4].wait_recv()
-    rs_out[5].wait_recv()
+    joined(0)
+    across(0, (2,), (16,))
+    joined(1)
+    across(2, (2, 3), (14, 18))
+    across(1, (2, 3), (15, 17))
+    across(3, (3,), (19,))
+
+    arrivals = ((6, 27, 20), (7, 5, 21), (4, 8, 22), (26, 9, 23))
     for n in (0, 2, 1, 3):
         rows = slice(n * TOK, (n + 1) * TOK)
         cols = slice(n * 512, (n + 1) * 512)
-        rs_out[6 + n].wait_recv()
-        rs_out[20 + n].wait_recv()
+        for number in arrivals[n]:
+            rs_out[number].wait_recv()
         total = attn_resid_ref[:, cols].astype(jnp.float32)
         for extra in (part_of(exp), full_in.at[0], full_in.at[1], far_in):
             total = total + extra[rows].astype(jnp.float32)
@@ -700,7 +711,7 @@
     hbm = pl.BlockSpec(memory_space=pl.ANY)
     dma = pltpu.SemaphoreType.DMA
     bf16, f32 = jnp.bfloat16, jnp.float32
-    counts = (7, 32, 3, 8, 8, 36, 36, 16, 16, 8, 8, 1, 1, 15, 15, 8, 8, 8, 8, 24, 24)
+    counts = (7, 32, 3, 8, 8, 36, 36, 16, 16, 8, 8, 1, 1, 15, 15, 8, 8, 8, 8, 28, 28)
     return pl.pallas_call(
         layer_kernel,
         out_shape=jax.ShapeDtypeStruct((2, TOK, D), bf16),
@@ -728,6 +739,7 @@
             pltpu.VMEM((4, 512, 512), bf16),
             pltpu.VMEM((512, 512), bf16),
             pltpu.VMEM((512, 512), bf16),
+            pltpu.VMEM((2, TOK, 512), bf16),
             pltpu.VMEM((2, TOK, D), bf16),
             pltpu.VMEM((2, TOK, D), bf16),
             pltpu.VMEM((TOK, FF), bf16),

time: 149 us -> 143 us (0.960)
  Pallas kernels: 146 us -> 138 us
    pallas_call x1, Pallas kernels: 146 us -> 138 us  [layer(): pl.pallas_call(layer_kernel, out_shape=jax.ShapeDtypeStruct((2, TOK, D),...]
where the time goes in v6:
time: 143 us; the launch traced here: 141 us
  Pallas kernels  138 us (97%)
  local copies, waits for them, and re-layouts  2.28 us (2%)
    pallas_call x1, Pallas kernels, layer(): pl.pallas_call(layer_kernel, out_shape=jax.ShapeDtypeStruct((2, TOK, D),...  138 us

profile of v6, /device:TPU:2, one launch (start us, length us, event | category | flops | bytes accessed | tf_op | source)
XLA Modules:
  0.0 141.3 jit_solution(3807694504870316430)
XLA Ops:
  0.6 138.4 %shard_map.122 = bf16[2,128,2048]{2,1,0:T(8,128)(2,1)} custom-call(bf16[128,4096]{1,0:T(8,128)(2,1)} %bitcast.11, bf16[128,512]{1,0:T(8,128)(2,1)} %bitcast.13, bf16[128,512]{1,0:T(8,128)(2,1)} %bitcast.14, bf16[128,2048]{1,0:T(8,128)(2,1)} %bitcast.12, bf16[512,128]{1,0:T(8,128)(2,1)} %weight_hbm.1, f32[1,2048]{1,0:T(1,128)} %bitcast.15, ...), custom_call_target="tpu_custom_call" | custom-call | tf_op jit(solution)/shard_map/pallas_call | solution.py:715
  139.0 2.3 %fusion = (bf16[1,128,2048]{2,1,0:T(8,128)(2,1)}, bf16[1,128,2048]{2,1,0:T(8,128)(2,1)}) fusion(bf16[2,128,2048]{2,1,0:T(8,128)(2,1)} %shard_map.122), kind=kLoop, calls=%fused_computation | loop fusion | bytes 2097152 | tf_op jit(solution)/shard_map/slice | solution.py:782
